TPU v7x, 512 devices: a whole 4x8x8 slice. The times are simulated.
512 devices in a mesh: zone: 32 (over x, z_hi, core), period: 16 (over y, z_lo).
Axes of the slice: x: 4, y: 8, z: 8 (z_hi: 4, z_lo: 2; z = z_hi * 2 + z_lo), core: 2. Of those that a mesh axis runs over, the one named last changes fastest.
Arguments:
- x_start: float32 [256, 16, 1600], P('zone', 'period'), may hold values from -6 to 6
- duals: float32 [256, 16, 512], P('zone', 'period'), may hold values from -3 to 3
- cost: float32 [256, 16, 1600], P('zone', 'period'), may hold values from -6 to 6
- hinv: bfloat16 [256, 1600, 1600], P('zone', 'period')
- zone_sizes: int32 [256], P('zone'), may hold values from 640 to 1600, as said below
- partners: int32 [4, 256], P(None, 'zone'), may hold values from 0 to 7, as said below
Outputs:
- primal: float32 [256, 16, 1600], P('zone', 'period')
- dual_out: float32 [256, 16, 512], P('zone', 'period')
Inputs may be any that keep to these rules, and one draw needn't show every extreme that they name: `zone_sizes`: each zone has at least its tie and ramp entries live; some zone uses all 1600. In round r the zones of zone index i are paired one to one with the zones of index i XOR 2**(r mod b), b the log2 of the number of zone indices; partners[r, z] is the partner's position among the 8 zones of its index, and the pairing is mutual.
All inputs are finite; a program needn't handle non-finite values.
Results may differ from a plain program's by a relative error of at most 0.0032.
Values may be sent and summed in bfloat16 or wider, within the bound.
No kernel may reach another device: no remote copies, remote signals or barrier semaphores. Data moves between devices by JAX's collectives and lax.ppermute only.
A program may use at most 64 MiB of HBM per device.

v0:
```python
import jax
import jax.numpy as jnp
from jax import lax
from jax.sharding import PartitionSpec as P

W = 128
G = 128
ROUNDS = 4
ITERS = 2


rho_ties = 1.0
prox_weight = 0.5
ramp_weight = 0.5


def from_partner(block, axis, apart):
    count = lax.axis_size(axis)
    route = []
    for low in range(count):
        high = low | 1 << apart
        if high != low and high < count:
            route += [(low, high), (high, low)]
    return lax.ppermute(block, axis, route)


def padded_2(cells, sides, width):
    for axis, dim in sides:
        count = lax.axis_size(axis)
        ends = count - 1
        head = lax.slice_in_dim(cells, 0, width, axis=dim)
        tail = lax.slice_in_dim(cells, cells.shape[dim] - width, cells.shape[dim], axis=dim)
        cells = jnp.concatenate(
            [
                lax.ppermute(tail, axis, [(i, (i + 1) % count) for i in range(ends)]),
                cells,
                lax.ppermute(head, axis, [((i + 1) % count, i) for i in range(ends)]),
            ],
            axis=dim,
        )
    return cells


def shards(x_start, duals, cost, hinv, zone_sizes, partners):
    zones_here = x_start.shape[0]
    width_total = x_start.shape[2]
    nbits = lax.axis_size("zone").bit_length() - 1
    live_mask = (lax.iota(jnp.int32, width_total)[None, :] < zone_sizes[:, None]).astype(
        jnp.float32
    )[:, None, :]
    tie_end = ROUNDS * W
    current = x_start
    dual_state = duals
    for iteration in range(ITERS):
        tie_terms = []
        new_duals = []
        for round_index in range(ROUNDS):
            own_block = current[:, :, round_index * W : (round_index + 1) * W]
            received = from_partner(own_block, "zone", round_index % nbits)
            partner_block = jnp.take(received, partners[round_index], axis=0)
            old_dual = dual_state[:, :, round_index * W : (round_index + 1) * W]
            updated = old_dual + rho_ties * 0.5 * (own_block - partner_block)
            new_duals.append(updated)
            tie_terms.append(rho_ties * 0.5 * (own_block + partner_block) - updated)
        dual_state = jnp.concatenate(new_duals, axis=2)
        ramp_block = current[:, :, tie_end : tie_end + G]
        padded = padded_2(ramp_block, (("period", 1),), 1)
        ramp_term = ramp_weight * (padded[:, 0:1] + padded[:, 2:3])
        filler = jnp.zeros((zones_here, 1, width_total - tie_end - G), jnp.float32)
        addition = jnp.concatenate(tie_terms + [ramp_term, filler], axis=2)
        right_side = ((prox_weight * current - cost + addition) * live_mask).astype(jnp.bfloat16)
        row_products = jnp.einsum(
            "zpv,zrv->zpr",
            lax.all_gather(right_side, "period", axis=1, tiled=True),
            hinv,
            preferred_element_type=jnp.float32,
        )
        product = lax.all_to_all(row_products, "period", split_axis=1, concat_axis=2, tiled=True)
        current = product * live_mask
    return (current, dual_state)


def solution(mesh):
    placed = (
        P("zone", "period", None),
        P("zone", "period", None),
        P("zone", "period", None),
        P("zone", "period", None),
        P("zone"),
        P(None, "zone"),
    )
    return jax.shard_map(
        shards,
        mesh=mesh,
        in_specs=placed,
        out_specs=(P("zone", "period", None), P("zone", "period", None)),
        check_vma=False,
    )
```

profile of v0, /device:TPU:6, one launch (start us, length us, event | category | flops | bytes accessed | tf_op | source)
XLA Modules:
  0.0 158.9 jit_solution(9922141693585990498)
XLA Ops:
  0.6 0.0 copy-start
  0.6 0.0 copy-start.2
  0.7 1.0 copy.10
  1.6 6.1 %collective-permute-start.1 = (f32[8,1,128]{2,0,1:T(8,128)S(1)}, f32[8,1,128]{2,0,1:T(8,128)S(1)}, u32[]{:S(2)}, u32[]{:S(2)}) collective-permute-start(f32[8,1,128]{2,0,1:T(8,128)S(1)} %get-tuple-element.30), channel_id=1, source_target_pairs={{0,32},{32,0},{16,48},{48,16},{64,96},{96,64},{80,112},{112,80},{1... | collective-permute-start | bytes 12296 | tf_op jit(solution)/shard_map/ppermute | solution.py:24
  7.7 1.9 %collective-permute-start = (f32[8,1,128]{2,0,1:T(8,128)S(1)}, f32[8,1,128]{2,0,1:T(8,128)S(1)}, u32[]{:S(2)}, u32[]{:S(2)}) collective-permute-start(f32[8,1,128]{2,0,1:T(8,128)S(1)} %get-tuple-element.31), channel_id=1, source_target_pairs={{0,16},{16,0},{32,48},{48,32},{64,80},{80,64},{96,112},{112,96},{1... | collective-permute-start | bytes 12296 | tf_op jit(solution)/shard_map/ppermute | solution.py:24
  9.6 0.8 compare_and_fusion
  10.5 0.7 fusion.11
  11.2 0.0 collective-permute-done.1
  11.3 0.6 gather_fusion.1
  11.8 0.0 collective-permute-done
  11.8 0.0 copy-start.1
  11.8 0.6 gather_fusion
  12.4 0.1 constant_dynamic-update-slice_fusion.5
  12.5 0.1 fusion.9
  12.5 2.7 %collective-permute-start.3 = (f32[8,1,128]{2,0,1:T(8,128)S(1)}, f32[8,1,128]{2,0,1:T(8,128)S(1)}, u32[]{:S(2)}, u32[]{:S(2)}) collective-permute-start(f32[8,1,128]{2,0,1:T(8,128)S(1)} %get-tuple-element.28), channel_id=1, source_target_pairs={{0,128},{128,0},{16,144},{144,16},{32,160},{160,32},{48,176},{176,... | collective-permute-start | bytes 12296 | tf_op jit(solution)/shard_map/ppermute | solution.py:24
  15.3 9.1 %collective-permute-start.2 = (f32[8,1,128]{2,0,1:T(8,128)S(1)}, f32[8,1,128]{2,0,1:T(8,128)S(1)}, u32[]{:S(2)}, u32[]{:S(2)}) collective-permute-start(f32[8,1,128]{2,0,1:T(8,128)S(1)} %get-tuple-element.29), channel_id=1, source_target_pairs={{0,64},{64,0},{16,80},{80,16},{32,96},{96,32},{48,112},{112,48},{1... | collective-permute-start | bytes 12296 | tf_op jit(solution)/shard_map/ppermute | solution.py:24
  24.4 1.3 collective-permute-start.5
  25.7 4.5 %collective-permute-start.4 = (f32[8,1,128]{2,0,1:T(8,128)S(1)}, f32[8,1,128]{2,0,1:T(8,128)S(1)}, u32[]{:S(2)}, u32[]{:S(2)}) collective-permute-start(f32[8,1,128]{2,0,1:T(8,128)S(1)} %get-tuple-element.26), channel_id=1, source_target_pairs={{0,1},{1,2},{2,3},{3,4},{4,5},{5,6},{6,7},{7,8},{8,9},{9,10},{10,1... | collective-permute-start | bytes 12296 | tf_op jit(solution)/shard_map/ppermute | solution.py:35
  30.3 0.0 collective-permute-done.3
  30.3 0.6 gather_fusion.3
  30.8 0.0 collective-permute-done.2
  30.9 0.6 gather_fusion.2
  31.4 0.1 constant_dynamic-update-slice_fusion.3
  31.5 0.1 constant_dynamic-update-slice_fusion.2
  31.6 0.0 collective-permute-done.5
  31.6 0.0 collective-permute-done.4
  31.6 0.9 select_convert_fusion.1
  32.5 37.4 %all_gather.6 = bf16[8,16,1600]{2,0,1:T(8,128)(2,1)S(1)} all-gather(bf16[8,1,1600]{2,0,1:T(8,128)(2,1)S(1)} %select_convert_fusion.1), channel_id=1, replica_groups=mesh['zone'=32,'period'=16] {'period'}, dimensions={1}, use_global_device_ids=true | all-gather | bytes 435200 | tf_op jit(solution)/shard_map/all_gather | solution.py:74
  69.9 0.0 copy-done
  69.9 0.9 fusion.2
  70.8 15.9 %all_to_all.24 = f32[8,16,100]{2,0,1:T(8,128)S(1)} all-to-all(f32[8,16,100]{2,0,1:T(8,128)S(1)} %copy.23), channel_id=1, replica_groups=mesh['zone'=32,'period'=16] {'period'}, dimensions={1} | all-to-all | bytes 102400 | tf_op jit(solution)/shard_map/all_to_all | solution.py:78
  86.7 0.1 all_to_all.9
  86.8 0.0 copy-done.2
  86.8 0.1 fusion.7
  86.9 2.9 %collective-permute-start.7 = (f32[8,1,128]{2,0,1:T(8,128)S(1)}, f32[8,1,128]{2,0,1:T(8,128)S(1)}, u32[]{:S(2)}, u32[]{:S(2)}) collective-permute-start(f32[8,1,128]{2,0,1:T(8,128)S(1)} %get-tuple-element.24), channel_id=1, source_target_pairs={{0,32},{32,0},{16,48},{48,16},{64,96},{96,64},{80,112},{112,80},{1... | collective-permute-start | bytes 12296 | tf_op jit(solution)/shard_map/ppermute | solution.py:24
  89.8 1.9 %collective-permute-start.6 = (f32[8,1,128]{2,0,1:T(8,128)S(1)}, f32[8,1,128]{2,0,1:T(8,128)S(1)}, u32[]{:S(2)}, u32[]{:S(2)}) collective-permute-start(f32[8,1,128]{2,0,1:T(8,128)S(1)} %get-tuple-element.25), channel_id=1, source_target_pairs={{0,16},{16,0},{32,48},{48,32},{64,80},{80,64},{96,112},{112,96},{1... | collective-permute-start | bytes 12296 | tf_op jit(solution)/shard_map/ppermute | solution.py:24
  91.8 1.6 collective-permute-done.7
  93.3 0.6 gather_fusion.5
  93.9 0.0 collective-permute-done.6
  93.9 0.6 gather_fusion.4
  94.4 0.1 constant_dynamic-update-slice_fusion.11
  94.5 0.1 constant_dynamic-update-slice_fusion.10
  94.6 3.1 %collective-permute-start.9 = (f32[8,1,128]{2,0,1:T(8,128)S(1)}, f32[8,1,128]{2,0,1:T(8,128)S(1)}, u32[]{:S(2)}, u32[]{:S(2)}) collective-permute-start(f32[8,1,128]{2,0,1:T(8,128)S(1)} %get-tuple-element.22), channel_id=1, source_target_pairs={{0,128},{128,0},{16,144},{144,16},{32,160},{160,32},{48,176},{176,... | collective-permute-start | bytes 12296 | tf_op jit(solution)/shard_map/ppermute | solution.py:24
  97.7 1.9 %collective-permute-start.8 = (f32[8,1,128]{2,0,1:T(8,128)S(1)}, f32[8,1,128]{2,0,1:T(8,128)S(1)}, u32[]{:S(2)}, u32[]{:S(2)}) collective-permute-start(f32[8,1,128]{2,0,1:T(8,128)S(1)} %get-tuple-element.23), channel_id=1, source_target_pairs={{0,64},{64,0},{16,80},{80,16},{32,96},{96,32},{48,112},{112,48},{1... | collective-permute-start | bytes 12296 | tf_op jit(solution)/shard_map/ppermute | solution.py:24
  99.6 1.3 collective-permute-start.11
  100.9 4.5 %collective-permute-start.10 = (f32[8,1,128]{2,0,1:T(8,128)S(1)}, f32[8,1,128]{2,0,1:T(8,128)S(1)}, u32[]{:S(2)}, u32[]{:S(2)}) collective-permute-start(f32[8,1,128]{2,0,1:T(8,128)S(1)} %get-tuple-element.21), channel_id=1, source_target_pairs={{0,1},{1,2},{2,3},{3,4},{4,5},{5,6},{6,7},{7,8},{8,9},{9,10},{10,1... | collective-permute-start | bytes 12296 | tf_op jit(solution)/shard_map/ppermute | solution.py:35
  105.5 0.0 collective-permute-done.9
  105.5 0.6 gather_fusion.7
  106.1 1.0 collective-permute-done.8
  107.1 0.6 gather_fusion.6
  107.7 0.1 constant_dynamic-update-slice_fusion.9
  107.7 0.1 constant_dynamic-update-slice_fusion.8
  107.8 0.0 collective-permute-done.11
  107.8 0.0 collective-permute-done.10
  107.9 0.1 select_convert_fusion
  108.0 33.2 %all_gather.7 = bf16[8,16,1600]{2,0,1:T(8,128)(2,1)S(1)} all-gather(bf16[8,1,1600]{2,0,1:T(8,128)(2,1)S(1)} %select_convert_fusion), channel_id=1, replica_groups=mesh['zone'=32,'period'=16] {'period'}, dimensions={1}, use_global_device_ids=true | all-gather | bytes 435200 | tf_op jit(solution)/shard_map/all_gather | solution.py:74
  141.2 0.9 fusion
  142.0 0.7 copy.28
  142.7 6.3 %all-to-all-start.1 = ((f32[8,16,100]{2,0,1:T(8,128)}), f32[8,16,100]{2,0,1:T(8,128)S(1)}, u32[]{:S(2)}, u32[]{:S(2)}) async-start(f32[8,16,100]{2,0,1:T(8,128)} %copy.28), calls=%async_computation.1 | async-start | bytes 131072 | tf_op jit(solution)/shard_map/all_to_all | solution.py:78
  149.0 0.6 copy.31
  149.6 8.4 %all-to-all-done.1 = f32[8,16,100]{2,0,1:T(8,128)S(1)} async-done(((f32[8,16,100]{2,0,1:T(8,128)}), f32[8,16,100]{2,0,1:T(8,128)S(1)}, u32[]{:S(2)}, u32[]{:S(2)}) %all-to-all-start.1) | async-done | bytes 51232 | tf_op jit(solution)/shard_map/all_to_all | solution.py:78
  158.1 0.1 all_to_all.21
  158.1 0.1 fusion.6
  158.2 0.7 copy.30
  (14 shorter events, 0.1 us)
Async XLA Ops:
  0.6 69.3 %copy-start = (bf16[8,100,1600]{2,0,1:T(8,128)(2,1)S(1)}, bf16[8,100,1600]{2,0,1:T(8,128)(2,1)}, u32[]{:S(2)}) copy-start(bf16[8,100,1600]{2,0,1:T(8,128)(2,1)} %param.11) | copy-start | bytes 7680004
  0.6 86.2 %copy-start.2 = (s32[8]{0:T(128)S(1)}, s32[8]{0:T(128)}, u32[]{:S(2)}) copy-start(s32[8]{0:T(128)} %param.12) | copy-start | bytes 100
  1.6 9.6 %collective-permute-start.1 = (f32[8,1,128]{2,0,1:T(8,128)S(1)}, f32[8,1,128]{2,0,1:T(8,128)S(1)}, u32[]{:S(2)}, u32[]{:S(2)}) collective-permute-start(f32[8,1,128]{2,0,1:T(8,128)S(1)} %get-tuple-element.30), channel_id=1, source_target_pairs={{0,32},{32,0},{16,48},{48,16},{64,96},{96,64},{80,112},{112,80},{1... | collective-permute-start | bytes 12296 | tf_op jit(solution)/shard_map/ppermute | solution.py:24
  7.7 4.1 %collective-permute-start = (f32[8,1,128]{2,0,1:T(8,128)S(1)}, f32[8,1,128]{2,0,1:T(8,128)S(1)}, u32[]{:S(2)}, u32[]{:S(2)}) collective-permute-start(f32[8,1,128]{2,0,1:T(8,128)S(1)} %get-tuple-element.31), channel_id=1, source_target_pairs={{0,16},{16,0},{32,48},{48,32},{64,80},{80,64},{96,112},{112,96},{1... | collective-permute-start | bytes 12296 | tf_op jit(solution)/shard_map/ppermute | solution.py:24
  11.8 96.0 %copy-start.1 = (f32[8,1,1600]{2,1,0:T(1,128)S(1)}, f32[8,1,1600]{2,1,0:T(1,128)}, u32[]{:S(2)}) copy-start(f32[8,1,1600]{2,1,0:T(1,128)} %param.10) | copy-start | bytes 153604
  12.5 17.7 %collective-permute-start.3 = (f32[8,1,128]{2,0,1:T(8,128)S(1)}, f32[8,1,128]{2,0,1:T(8,128)S(1)}, u32[]{:S(2)}, u32[]{:S(2)}) collective-permute-start(f32[8,1,128]{2,0,1:T(8,128)S(1)} %get-tuple-element.28), channel_id=1, source_target_pairs={{0,128},{128,0},{16,144},{144,16},{32,160},{160,32},{48,176},{176,... | collective-permute-start | bytes 12296 | tf_op jit(solution)/shard_map/ppermute | solution.py:24
  15.3 15.6 %collective-permute-start.2 = (f32[8,1,128]{2,0,1:T(8,128)S(1)}, f32[8,1,128]{2,0,1:T(8,128)S(1)}, u32[]{:S(2)}, u32[]{:S(2)}) collective-permute-start(f32[8,1,128]{2,0,1:T(8,128)S(1)} %get-tuple-element.29), channel_id=1, source_target_pairs={{0,64},{64,0},{16,80},{80,16},{32,96},{96,32},{48,112},{112,48},{1... | collective-permute-start | bytes 12296 | tf_op jit(solution)/shard_map/ppermute | solution.py:24
  24.4 7.1 %collective-permute-start.5 = (f32[8,1,128]{2,0,1:T(8,128)S(1)}, f32[8,1,128]{2,0,1:T(8,128)S(1)}, u32[]{:S(2)}, u32[]{:S(2)}) collective-permute-start(f32[8,1,128]{2,0,1:T(8,128)S(1)} %get-tuple-element.26), channel_id=1, source_target_pairs={{1,0},{2,1},{3,2},{4,3},{5,4},{6,5},{7,6},{8,7},{9,8},{10,9},{11,1... | collective-permute-start | bytes 12296 | tf_op jit(solution)/shard_map/ppermute | solution.py:37
  25.7 5.9 %collective-permute-start.4 = (f32[8,1,128]{2,0,1:T(8,128)S(1)}, f32[8,1,128]{2,0,1:T(8,128)S(1)}, u32[]{:S(2)}, u32[]{:S(2)}) collective-permute-start(f32[8,1,128]{2,0,1:T(8,128)S(1)} %get-tuple-element.26), channel_id=1, source_target_pairs={{0,1},{1,2},{2,3},{3,4},{4,5},{5,6},{6,7},{7,8},{8,9},{9,10},{10,1... | collective-permute-start | bytes 12296 | tf_op jit(solution)/shard_map/ppermute | solution.py:35
  86.9 6.4 %collective-permute-start.7 = (f32[8,1,128]{2,0,1:T(8,128)S(1)}, f32[8,1,128]{2,0,1:T(8,128)S(1)}, u32[]{:S(2)}, u32[]{:S(2)}) collective-permute-start(f32[8,1,128]{2,0,1:T(8,128)S(1)} %get-tuple-element.24), channel_id=1, source_target_pairs={{0,32},{32,0},{16,48},{48,16},{64,96},{96,64},{80,112},{112,80},{1... | collective-permute-start | bytes 12296 | tf_op jit(solution)/shard_map/ppermute | solution.py:24
  89.8 4.1 %collective-permute-start.6 = (f32[8,1,128]{2,0,1:T(8,128)S(1)}, f32[8,1,128]{2,0,1:T(8,128)S(1)}, u32[]{:S(2)}, u32[]{:S(2)}) collective-permute-start(f32[8,1,128]{2,0,1:T(8,128)S(1)} %get-tuple-element.25), channel_id=1, source_target_pairs={{0,16},{16,0},{32,48},{48,32},{64,80},{80,64},{96,112},{112,96},{1... | collective-permute-start | bytes 12296 | tf_op jit(solution)/shard_map/ppermute | solution.py:24
  94.6 10.9 %collective-permute-start.9 = (f32[8,1,128]{2,0,1:T(8,128)S(1)}, f32[8,1,128]{2,0,1:T(8,128)S(1)}, u32[]{:S(2)}, u32[]{:S(2)}) collective-permute-start(f32[8,1,128]{2,0,1:T(8,128)S(1)} %get-tuple-element.22), channel_id=1, source_target_pairs={{0,128},{128,0},{16,144},{144,16},{32,160},{160,32},{48,176},{176,... | collective-permute-start | bytes 12296 | tf_op jit(solution)/shard_map/ppermute | solution.py:24
  97.7 9.4 %collective-permute-start.8 = (f32[8,1,128]{2,0,1:T(8,128)S(1)}, f32[8,1,128]{2,0,1:T(8,128)S(1)}, u32[]{:S(2)}, u32[]{:S(2)}) collective-permute-start(f32[8,1,128]{2,0,1:T(8,128)S(1)} %get-tuple-element.23), channel_id=1, source_target_pairs={{0,64},{64,0},{16,80},{80,16},{32,96},{96,32},{48,112},{112,48},{1... | collective-permute-start | bytes 12296 | tf_op jit(solution)/shard_map/ppermute | solution.py:24
  99.6 8.2 %collective-permute-start.11 = (f32[8,1,128]{2,0,1:T(8,128)S(1)}, f32[8,1,128]{2,0,1:T(8,128)S(1)}, u32[]{:S(2)}, u32[]{:S(2)}) collective-permute-start(f32[8,1,128]{2,0,1:T(8,128)S(1)} %get-tuple-element.21), channel_id=1, source_target_pairs={{1,0},{2,1},{3,2},{4,3},{5,4},{6,5},{7,6},{8,7},{9,8},{10,9},{11,1... | collective-permute-start | bytes 12296 | tf_op jit(solution)/shard_map/ppermute | solution.py:37
  100.9 6.9 %collective-permute-start.10 = (f32[8,1,128]{2,0,1:T(8,128)S(1)}, f32[8,1,128]{2,0,1:T(8,128)S(1)}, u32[]{:S(2)}, u32[]{:S(2)}) collective-permute-start(f32[8,1,128]{2,0,1:T(8,128)S(1)} %get-tuple-element.21), channel_id=1, source_target_pairs={{0,1},{1,2},{2,3},{3,4},{4,5},{5,6},{6,7},{7,8},{8,9},{9,10},{10,1... | collective-permute-start | bytes 12296 | tf_op jit(solution)/shard_map/ppermute | solution.py:35
  142.7 15.3 %all-to-all-start.1 = ((f32[8,16,100]{2,0,1:T(8,128)}), f32[8,16,100]{2,0,1:T(8,128)S(1)}, u32[]{:S(2)}, u32[]{:S(2)}) async-start(f32[8,16,100]{2,0,1:T(8,128)} %copy.28), calls=%async_computation.1 | async-start | bytes 131072 | tf_op jit(solution)/shard_map/all_to_all | solution.py:78
where the time goes:
time: 160 us; the launch traced here: 159 us
  blocking collectives  86.5 us (54%)
  starting transfers between devices  47.6 us (30%)
  waiting for transfers between devices  11.1 us (7%)
  local copies, waits for them, and re-layouts  8.4 us (5%)
  other arithmetic  2.66 us (2%)
  matrix products  1.75 us (1%)
    all_gather x2, blocking collectives, shards(): lax.all_gather(right_side, 'period', axis=1, tiled=True)  70.6 us
    ppermute x8, starting transfers between devices, from_partner(): return lax.ppermute(block, axis, route)  29.7 us
    all_to_all x1, blocking collectives, shards(): lax.all_to_all(row_products, 'period', split_axis=1, concat_axis=2, tiled...  15.9 us
    ppermute x2, starting transfers between devices, padded_2(): lax.ppermute(tail, axis, [(i, (i + 1) % count) for i in range(ends)])  9.09 us
    all_to_all x1, waiting for transfers between devices, shards(): lax.all_to_all(row_products, 'period', split_axis=1, concat_axis=2, tiled...  8.41 us
    all_to_all x1, starting transfers between devices, shards(): lax.all_to_all(row_products, 'period', split_axis=1, concat_axis=2, tiled...  6.28 us
    gather x8, local copies, waits for them, and re-layouts, shards(): partner_block = jnp.take(received, partners[round_index], axis=0)  4.44 us
  transfers between devices with their start and end apart: 13, of which 3 were waited for; matrix products, arithmetic and copies ran while one was open for 4% of the time, Pallas kernels for 0%

commit v1 on v0

v1 whole, which is shorter than its diff:
```python
import functools
import itertools

import jax
import jax.numpy as jnp
from jax import lax
from jax.experimental import pallas as pl
from jax.experimental.pallas import tpu as pltpu
from jax.sharding import Mesh, PartitionSpec as P

V = 1600
W = 128
ROUNDS = 4
TIE = ROUNDS * W
RAMP = TIE + W
Z = 8
T = 16
ROWS = V // T
VP = 1664
BW = VP + 3 * W
DW = VP + 2 * W
AXES = ("xh", "xl", "zh", "core", "y", "zl")
SIZES = (2, 2, 4, 2, 8, 2)
ZONE = ("xh", "xl", "zh", "core")
NEAR = ("xl", "zh", "core")
PERIOD = ("y", "zl")
FIRST = {0: 0, 1: 1, 2: 2, 3: 2, 4: 3, 5: 3}
SECOND = {1: 0, 2: 1, 3: 3}


def near_index():
    return (lax.axis_index("xl") * 4 + lax.axis_index("zh")) * 2 + lax.axis_index("core")


def period_index():
    return lax.axis_index("y") * 2 + lax.axis_index("zl")


def swap_route(rounds):
    route = []
    for place in itertools.product(*[range(size) for size in SIZES]):
        xh, xl, zh, core, y, zl = place
        k = y * 2 + zl
        if k in rounds:
            zone = ((xh * 2 + xl) * 4 + zh) * 2 + core
            mate = zone ^ (1 << rounds[k])
            there = (mate >> 4, (mate >> 3) & 1, (mate >> 1) & 3, mate & 1, y, zl)
            ends = []
            for spot in (place, there):
                flat = 0
                for size, index in zip(SIZES, spot):
                    flat = flat * size + index
                ends.append(flat)
            route.append(tuple(ends))
    return route


def rounded(values):
    return values.astype(jnp.bfloat16)


def two_parts(values):
    high = rounded(values)
    return high, rounded(values - high.astype(jnp.float32))


def tie_blocks_kernel(x_ref, out_ref):
    me = near_index()
    out_ref[...] = jnp.zeros_like(out_ref)
    x = x_ref[:, 0, :TIE]
    for r in range(ROUNDS):
        slot = pl.multiple_of((me ^ (1 << r)) * Z, Z)
        out_ref[pl.ds(slot, Z), :] = x[:, r * W : (r + 1) * W]


def first_side_kernel(sizes_ref, partners_ref, x_ref, dual_ref, cost_ref, ties_ref, out_ref, dual_out_ref):
    me = near_index()
    x = x_ref[:, 0, :]
    cost = cost_ref[:, 0, :]
    dual = dual_ref[:, 0, :]
    lane = lax.broadcasted_iota(jnp.int32, (1, V), 1)
    live = jnp.concatenate([(lane < sizes_ref[z]).astype(jnp.float32) for z in range(Z)], axis=0)
    terms, new_duals = [], []
    for r in range(ROUNDS):
        own = x[:, r * W : (r + 1) * W]
        slot = (me ^ (1 << r)) * Z
        other = jnp.concatenate([ties_ref[pl.ds(slot + partners_ref[r, z], 1), :] for z in range(Z)], axis=0)
        updated = dual[:, r * W : (r + 1) * W] + 0.5 * (own - other)
        new_duals.append(updated)
        terms.append(0.5 * (own + other) - updated)
    new_dual = jnp.concatenate(new_duals, axis=1)
    rest = jnp.zeros((Z, V - TIE), jnp.float32)
    right = (0.5 * x - cost + jnp.concatenate(terms + [rest], axis=1)) * live
    dual_out_ref[...] = new_dual
    later = cost + jnp.concatenate([new_dual, rest], axis=1)
    later_high, later_low = two_parts(later)
    common = jnp.concatenate(
        [rounded(right), jnp.zeros((Z, VP - V), jnp.bfloat16), rounded(x[:, TIE:RAMP])], axis=1
    )
    blank = jnp.zeros((Z, W - ROWS), jnp.bfloat16)
    for k in range(T):
        own_rows = slice(k * ROWS, (k + 1) * ROWS)
        out_ref[k * Z : (k + 1) * Z, :] = jnp.concatenate(
            [common, later_high[:, own_rows], blank, later_low[:, own_rows], blank], axis=1
        )


def next_period(values):
    edge = jnp.zeros((Z, values.shape[1]), values.dtype)
    return jnp.concatenate([values[Z:], edge], axis=0)


def last_period(values):
    edge = jnp.zeros((Z, values.shape[1]), values.dtype)
    return jnp.concatenate([edge, values[:-Z]], axis=0)


def first_product_kernel(sizes_ref, block_ref, hinv_ref, out_ref):
    first = period_index() * ROWS
    ramp = block_ref[:, VP : VP + W].astype(jnp.float32)
    ramp_side = block_ref[:, TIE:RAMP].astype(jnp.float32) + 0.5 * (last_period(ramp) + next_period(ramp))
    side = jnp.concatenate([block_ref[:, :TIE], rounded(ramp_side), block_ref[:, RAMP:V]], axis=1)
    row = lax.broadcasted_iota(jnp.int32, (T * Z, ROWS), 0) & (Z - 1)
    lane = lax.broadcasted_iota(jnp.int32, (T * Z, ROWS), 1) + first
    total = jnp.zeros((T * Z, ROWS), jnp.float32)
    for z in range(Z):
        product = lax.dot_general(
            side, hinv_ref[z], (((1,), (1,)), ((), ())), preferred_element_type=jnp.float32
        )
        total = jnp.where((row == z) & (lane < sizes_ref[z]), product, total)
    out_ref[...] = jnp.concatenate([total, jnp.zeros((T * Z, W - ROWS), jnp.float32)], axis=1)


def second_product_kernel(sizes_ref, partners_ref, block_ref, current_ref, one_ref, two_ref, hinv_ref, out_ref):
    k = period_index()
    first = k * ROWS
    first_round = jnp.where(k == 0, 0, jnp.where(k == 1, 1, jnp.where(k <= 3, 2, 3)))
    second_round = jnp.where(k == 1, 0, jnp.where(k == 2, 1, jnp.where(k == 3, 3, 0)))
    current = current_ref[...]
    later = block_ref[:, VP + W : VP + 2 * W].astype(jnp.float32) + block_ref[:, VP + 2 * W :].astype(jnp.float32)
    zone = lax.broadcasted_iota(jnp.int32, (Z, W), 0)
    column = lax.broadcasted_iota(jnp.int32, (Z, W), 1)

    def from_partner(received_ref, round_index):
        partner = jnp.zeros((Z, W), jnp.int32)
        for z in range(Z):
            partner = jnp.where(zone == z, partners_ref[round_index, z], partner)
        pick = jnp.concatenate(
            [(column - p * Z == partner).astype(jnp.float32) for p in range(T)], axis=0
        )
        return jnp.dot(
            pick, received_ref[...], preferred_element_type=jnp.float32, precision=lax.Precision.HIGHEST
        )

    row = lax.broadcasted_iota(jnp.int32, (T * Z, W), 0) & (Z - 1)
    lane = lax.broadcasted_iota(jnp.int32, (T * Z, W), 1)
    entry = lane + first
    round_of = entry >> 7
    tie = entry < TIE
    other = jnp.where(
        round_of == first_round,
        from_partner(one_ref, first_round),
        from_partner(two_ref, second_round),
    )
    ramp = 0.5 * (last_period(current) + next_period(current))
    addition = jnp.where(tie, other, jnp.where(entry < RAMP, ramp, 0.0))
    right = 0.5 * current - later + addition
    size = jnp.zeros((T * Z, W), jnp.int32)
    for z in range(Z):
        size = jnp.where(row == z, sizes_ref[z], size)
    right = rounded(jnp.where((entry < size) & (lane < ROWS), right, 0.0))[:, :ROWS]
    step_high, step_low = two_parts(jnp.where(tie, 0.5 * (current - other), 0.0))
    out_ref[:, VP : VP + W] = step_high
    out_ref[:, VP + W :] = step_low
    row = row[:, :ROWS]
    total = jnp.zeros((T * Z, V), jnp.float32)
    for z in range(Z):
        total = total + jnp.dot(
            jnp.where(row == z, right, jnp.zeros_like(right)), hinv_ref[z], preferred_element_type=jnp.float32
        )
    out_ref[:, :V] = rounded(total)
    out_ref[:, V:VP] = jnp.zeros((T * Z, VP - V), jnp.bfloat16)


def last_sum_kernel(sizes_ref, block_ref, dual_ref, primal_ref, dual_out_ref):
    lane = lax.broadcasted_iota(jnp.int32, (1, V), 1)
    live = jnp.concatenate([(lane < sizes_ref[z]).astype(jnp.float32) for z in range(Z)], axis=0)
    total = jnp.zeros((Z, V), jnp.float32)
    for k in range(T):
        total = total + block_ref[k * Z : (k + 1) * Z, :V].astype(jnp.float32)
    primal_ref[:, 0, :] = total * live
    steps = []
    for k in range(-(-TIE // ROWS)):
        part = block_ref[k * Z : (k + 1) * Z, VP : VP + W].astype(jnp.float32) + block_ref[
            k * Z : (k + 1) * Z, VP + W :
        ].astype(jnp.float32)
        steps.append(part[:, : min(ROWS, TIE - k * ROWS)])
    dual_out_ref[:, 0, :] = dual_ref[...] + jnp.concatenate(steps, axis=1)


SMEM = pl.BlockSpec(memory_space=pltpu.SMEM)
VMEM = pl.BlockSpec(memory_space=pltpu.VMEM)


def call(kernel, name, in_specs, out_shape):
    many = isinstance(out_shape, tuple)
    return pl.pallas_call(
        kernel,
        name=name,
        in_specs=in_specs,
        out_specs=tuple(VMEM for _ in out_shape) if many else VMEM,
        out_shape=out_shape,
    )


def shards(x, duals, cost, hinv, sizes, partners):
    shape = jax.ShapeDtypeStruct
    f32, bf16 = jnp.float32, jnp.bfloat16
    ties = call(tie_blocks_kernel, "tie_blocks", [VMEM], shape((T * Z, W), f32))(x)
    ties = lax.all_to_all(ties, NEAR, 0, 0, tiled=True)
    block, dual = call(
        first_side_kernel,
        "first_side",
        [SMEM, SMEM, VMEM, VMEM, VMEM, VMEM],
        (shape((T * Z, BW), bf16), shape((Z, TIE), f32)),
    )(sizes, partners, x, duals, cost, ties)
    block = lax.all_to_all(block, PERIOD, 0, 0, tiled=True)
    current = call(first_product_kernel, "first_product", [SMEM, VMEM, VMEM], shape((T * Z, W), f32))(
        sizes, block, hinv
    )
    one = lax.ppermute(current, AXES, swap_route(FIRST))
    two = lax.ppermute(current, AXES, swap_route(SECOND))
    block = call(
        second_product_kernel,
        "second_product",
        [SMEM, SMEM, VMEM, VMEM, VMEM, VMEM, VMEM],
        shape((T * Z, DW), bf16),
    )(sizes, partners, block, current, one, two, hinv)
    block = lax.all_to_all(block, PERIOD, 0, 0, tiled=True)
    return call(
        last_sum_kernel, "last_sum", [SMEM, VMEM, VMEM], (shape((Z, 1, V), f32), shape((Z, 1, TIE), f32))
    )(sizes, block, dual)


def solution(mesh):
    fine = Mesh(mesh.devices.reshape(SIZES), AXES)
    whole = P(ZONE, PERIOD, None)
    return jax.shard_map(
        shards,
        mesh=fine,
        in_specs=(whole, whole, whole, whole, P(ZONE), P(None, ZONE)),
        out_specs=(whole, whole),
        check_vma=False,
    )
```

time: 160 us -> 90.6 us (0.57)
  blocking collectives: 86.5 us -> 44.5 us
  starting transfers between devices: 47.6 us -> 10.6 us
  Pallas kernels: 0 us -> 13 us
  waiting for transfers between devices: 11.1 us -> 15.7 us
  local copies, waits for them, and re-layouts: 8.4 us -> 5.04 us
  other arithmetic: 2.66 us -> 0 us
  matrix products: 1.75 us -> 0 us
    all_gather x2 -> x0, blocking collectives: 70.6 us -> none  [shards(): lax.all_gather(right_side, 'period', axis=1, tiled=True)]
    ppermute x12 -> x2, starting transfers between devices: 41.4 us -> 2.57 us  [the longest x1 1.92 us: shards(): one = lax.ppermute(current, AXES, swap_route(FIRST))]
    all_to_all x1 -> x2, blocking collectives: 15.9 us -> 44.5 us  [the longest x1 25.2 us: shards(): block = lax.all_to_all(block, PERIOD, 0, 0, tiled=True)]
    pallas_call x0 -> x5, Pallas kernels: none -> 13 us  [the longest x1 4.16 us: shards(): call(second_product_kernel, 'second_product', [SMEM, SMEM, VMEM, VMEM, VM...]
    all_to_all x1, waiting for transfers between devices: 8.41 us -> 14.3 us  [shards(): block = lax.all_to_all(block, PERIOD, 0, 0, tiled=True)]
    gather x8 -> x0, local copies, waits for them, and re-layouts: 4.44 us -> none  [shards(): partner_block = jnp.take(received, partners[round_index], axis=0)]
    unnamed x9 -> x7, local copies, waits for them, and re-layouts: 2.29 us -> 5.04 us
    dot_general x2 -> x0, matrix products: 1.75 us -> none  [shards(): jnp.einsum('zpv,zrv->zpr', lax.all_gather(right_side, 'period', axis=1, t...]
  transfers between devices with their start and end apart: 13 -> 3, of which waited for: 3 -> 2; matrix products, arithmetic and copies ran while one was open for 4% -> 4% of each run, Pallas kernels for 0% -> 0%
where the time goes in v1:
time: 90.6 us; the launch traced here: 89.6 us
  blocking collectives  44.5 us (49%)
  waiting for transfers between devices  15.7 us (17%)
  Pallas kernels  13 us (14%)
  starting transfers between devices  10.6 us (12%)
  local copies, waits for them, and re-layouts  5.04 us (6%)
    all_to_all x1, blocking collectives, shards(): block = lax.all_to_all(block, PERIOD, 0, 0, tiled=True)  25.2 us
    all_to_all x1, blocking collectives, shards(): ties = lax.all_to_all(ties, NEAR, 0, 0, tiled=True)  19.3 us
    all_to_all x1, waiting for transfers between devices, shards(): block = lax.all_to_all(block, PERIOD, 0, 0, tiled=True)  14.3 us
    all_to_all x1, starting transfers between devices, shards(): block = lax.all_to_all(block, PERIOD, 0, 0, tiled=True)  8 us
    unnamed x7, local copies, waits for them, and re-layouts  5.04 us
    pallas_call x1, Pallas kernels, shards(): call(second_product_kernel, 'second_product', [SMEM, SMEM, VMEM, VMEM, VM...  4.16 us
    pallas_call x1, Pallas kernels, shards(): call(first_product_kernel, 'first_product', [SMEM, VMEM, VMEM], shape((T...  3.68 us
    pallas_call x1, Pallas kernels, shards(): call(first_side_kernel, 'first_side', [SMEM, SMEM, VMEM, VMEM, VMEM, VMEM...  1.94 us
  transfers between devices with their start and end apart: 3, of which 2 were waited for; matrix products, arithmetic and copies ran while one was open for 4% of the time, Pallas kernels for 0%

profile of v1, /device:TPU:6, one launch (start us, length us, event | category | flops | bytes accessed | tf_op | source)
XLA Modules:
  0.0 89.6 jit_solution(6970873454916075043)
XLA Ops:
  0.6 1.4 %tie_blocks.1 = f32[128,128]{1,0:T(8,128)} custom-call(f32[8,1,1600]{2,1,0:T(1,128)} %x_ref.3), custom_call_target="tpu_custom_call" | custom-call | tf_op jit(solution)/shard_map/tie_blocks/pallas_call | solution.py:219
  2.1 19.3 %all_to_all.33 = f32[16,8,128]{2,1,0:T(8,128)} all-to-all(f32[16,8,128]{2,1,0:T(8,128)} %bitcast.12), channel_id=1, replica_groups=mesh['xh'=2,'xl'=2,'zh'=4,'core'=2,'y'=8,'zl'=2] {'xl','zh','core'}, dimensions={0} | all-to-all | bytes 131072 | tf_op jit(solution)/shard_map/all_to_all | solution.py:220
  21.3 1.9 %first_side.1 = (bf16[128,2048]{1,0:T(8,128)(2,1)}, f32[8,512]{1,0:T(8,128)}) custom-call(s32[8]{0:T(128)} %sizes_ref.7, s32[4,8]{1,0:T(4,128)} %partners_ref.3, f32[8,1,1600]{2,1,0:T(1,128)} %x_ref.3, f32[8,1,512]{2,1,0:T(1,128)} %dual_ref.1, f32[8,1,1600]{2,1,0:T(1,128)} %cost_ref.1, f32[128,128]{1,0:T(8,128)} %bitcast.11), custom_call_target="tpu_custom_call" | custom-call | tf_op jit(solution)/shard_map/first_side/pallas_call | solution.py:221
  23.3 8.0 %all-to-all-start.1 = ((bf16[16,8,2048]{2,1,0:T(8,128)(2,1)}), bf16[16,8,2048]{2,1,0:T(8,128)(2,1)S(1)}, u32[]{:S(2)}, u32[]{:S(2)}) async-start(bf16[16,8,2048]{2,1,0:T(8,128)(2,1)} %bitcast.10), calls=%async_computation.1 | async-start | bytes 1048576 | tf_op jit(solution)/shard_map/all_to_all | solution.py:227
  31.3 3.6 %copy.8.hinv_ref = bf16[8,100,1600]{2,1,0:T(8,128)(2,1)} copy(bf16[8,100,1600]{2,0,1:T(8,128)(2,1)} %param.9) | data formatting | bytes 5120000 | tf_op args[3]
  34.9 14.3 %all-to-all-done.1 = bf16[16,8,2048]{2,1,0:T(8,128)(2,1)S(1)} async-done(((bf16[16,8,2048]{2,1,0:T(8,128)(2,1)}), bf16[16,8,2048]{2,1,0:T(8,128)(2,1)S(1)}, u32[]{:S(2)}, u32[]{:S(2)}) %all-to-all-start.1) | async-done | bytes 524320 | tf_op jit(solution)/shard_map/all_to_all | solution.py:227
  49.2 0.0 copy-start
  49.2 0.8 copy-done
  50.0 3.7 %first_product.1.current_ref = f32[128,128]{1,0:T(8,128)} custom-call(s32[8]{0:T(128)} %sizes_ref.7, bf16[128,2048]{1,0:T(8,128)(2,1)} %bitcast.6, bf16[8,100,1600]{2,1,0:T(8,128)(2,1)} %copy.8.hinv_ref), custom_call_target="tpu_custom_call" | custom-call | tf_op jit(solution)/shard_map/first_product/pallas_call | solution.py:228
  53.7 0.7 collective-permute-start.1
  54.4 1.9 %collective-permute-start = (f32[128,128]{1,0:T(8,128)}, f32[128,128]{1,0:T(8,128)S(1)}, u32[]{:S(2)}, u32[]{:S(2)}) collective-permute-start(f32[128,128]{1,0:T(8,128)} %first_product.1.current_ref), channel_id=1, source_target_pairs={{0,16},{1,33},{2,66},{3,67},{4,132},{5,133},{16,0},{17,49},{18,82}... | collective-permute-start | bytes 196616 | tf_op jit(solution)/shard_map/ppermute | solution.py:231
  56.3 0.0 collective-permute-done.1.two_ref
  56.3 0.0 copy-start.1
  56.3 1.4 %collective-permute-done.one_ref = f32[128,128]{1,0:T(8,128)S(1)} collective-permute-done((f32[128,128]{1,0:T(8,128)}, f32[128,128]{1,0:T(8,128)S(1)}, u32[]{:S(2)}, u32[]{:S(2)}) %collective-permute-start) | collective-permute-done | bytes 65568 | tf_op jit(solution)/shard_map/ppermute | solution.py:231
  57.7 0.0 copy-done.1
  57.7 0.0 copy-start.2
  57.7 0.6 copy-done.2
  58.4 4.2 %second_product.1 = bf16[128,1920]{1,0:T(8,128)(2,1)} custom-call(s32[8]{0:T(128)} %sizes_ref.7, s32[4,8]{1,0:T(4,128)} %partners_ref.3, bf16[128,2048]{1,0:T(8,128)(2,1)} %bitcast.7, f32[128,128]{1,0:T(8,128)} %first_product.1.current_ref, f32[128,128]{1,0:T(8,128)} %copy-done.2, f32[128,128]{1,0:T(8,128)} %copy-done.1, bf16[8,100,1600]{2,1,0:T(8,128)(2,1)} %copy.8.hinv_ref), custom_call_target="tpu_custom_call" | custom-call | tf_op jit(solution)/shard_map/second_product/pallas_call | solution.py:233
  62.5 25.2 %all_to_all.34 = bf16[16,8,1920]{2,1,0:T(8,128)(2,1)} all-to-all(bf16[16,8,1920]{2,1,0:T(8,128)(2,1)} %bitcast.9), channel_id=1, replica_groups=mesh['xh'=2,'xl'=2,'zh'=4,'core'=2,'y'=8,'zl'=2] {'y','zl'}, dimensions={0} | all-to-all | bytes 983040 | tf_op jit(solution)/shard_map/all_to_all | solution.py:239
  87.8 1.8 %last_sum.1 = (f32[8,1,1600]{2,1,0:T(1,128)}, f32[8,1,512]{2,1,0:T(1,128)}) custom-call(s32[8]{0:T(128)} %sizes_ref.7, bf16[128,1920]{1,0:T(8,128)(2,1)} %bitcast.8, f32[8,512]{1,0:T(8,128)} %get-tuple-element.5.dual_ref), custom_call_target="tpu_custom_call" | custom-call | tf_op jit(solution)/shard_map/last_sum/pallas_call | solution.py:240
Async XLA Ops:
  23.3 25.9 %all-to-all-start.1 = ((bf16[16,8,2048]{2,1,0:T(8,128)(2,1)}), bf16[16,8,2048]{2,1,0:T(8,128)(2,1)S(1)}, u32[]{:S(2)}, u32[]{:S(2)}) async-start(bf16[16,8,2048]{2,1,0:T(8,128)(2,1)} %bitcast.10), calls=%async_computation.1 | async-start | bytes 1048576 | tf_op jit(solution)/shard_map/all_to_all | solution.py:227
  49.2 0.8 copy-start
  53.7 2.6 %collective-permute-start.1 = (f32[128,128]{1,0:T(8,128)}, f32[128,128]{1,0:T(8,128)S(1)}, u32[]{:S(2)}, u32[]{:S(2)}) collective-permute-start(f32[128,128]{1,0:T(8,128)} %first_product.1.current_ref), channel_id=1, source_target_pairs={{1,17},{2,34},{3,131},{17,1},{18,50},{19,147},{33,49},{34,2},{35,1... | collective-permute-start | bytes 196616 | tf_op jit(solution)/shard_map/ppermute | solution.py:232
  54.4 3.4 %collective-permute-start = (f32[128,128]{1,0:T(8,128)}, f32[128,128]{1,0:T(8,128)S(1)}, u32[]{:S(2)}, u32[]{:S(2)}) collective-permute-start(f32[128,128]{1,0:T(8,128)} %first_product.1.current_ref), channel_id=1, source_target_pairs={{0,16},{1,33},{2,66},{3,67},{4,132},{5,133},{16,0},{17,49},{18,82}... | collective-permute-start | bytes 196616 | tf_op jit(solution)/shard_map/ppermute | solution.py:231
  56.3 1.4 %copy-start.1 = (f32[128,128]{1,0:T(8,128)}, f32[128,128]{1,0:T(8,128)S(1)}, u32[]{:S(2)}) copy-start(f32[128,128]{1,0:T(8,128)S(1)} %collective-permute-done.1.two_ref) | copy-start | bytes 196612
  57.7 0.6 copy-start.2

commit v2 on v1

--- a/solution.py
+++ b/solution.py
@@ -210,33 +210,39 @@
         in_specs=in_specs,
         out_specs=tuple(VMEM for _ in out_shape) if many else VMEM,
         out_shape=out_shape,
-    )
+        compiler_params=pltpu.CompilerParams(vmem_limit_bytes=16 << 20),
+    )
+
+
+def near(values):
+    return pltpu.with_memory_space_constraint(values, pltpu.VMEM)
 
 
 def shards(x, duals, cost, hinv, sizes, partners):
-    shape = jax.ShapeDtypeStruct
     f32, bf16 = jnp.float32, jnp.bfloat16
-    ties = call(tie_blocks_kernel, "tie_blocks", [VMEM], shape((T * Z, W), f32))(x)
-    ties = lax.all_to_all(ties, NEAR, 0, 0, tiled=True)
+    x, duals, cost, hinv = near(x), near(duals), near(cost), near(hinv)
+    ties = call(tie_blocks_kernel, "tie_blocks", [VMEM], pltpu.VMEM((T * Z, W), f32))(x)
+    ties = near(lax.all_to_all(ties, NEAR, 0, 0, tiled=True))
     block, dual = call(
         first_side_kernel,
         "first_side",
         [SMEM, SMEM, VMEM, VMEM, VMEM, VMEM],
-        (shape((T * Z, BW), bf16), shape((Z, TIE), f32)),
+        (pltpu.VMEM((T * Z, BW), bf16), pltpu.VMEM((Z, TIE), f32)),
     )(sizes, partners, x, duals, cost, ties)
-    block = lax.all_to_all(block, PERIOD, 0, 0, tiled=True)
-    current = call(first_product_kernel, "first_product", [SMEM, VMEM, VMEM], shape((T * Z, W), f32))(
+    block = near(lax.all_to_all(block, PERIOD, 0, 0, tiled=True))
+    current = call(first_product_kernel, "first_product", [SMEM, VMEM, VMEM], pltpu.VMEM((T * Z, W), f32))(
         sizes, block, hinv
     )
-    one = lax.ppermute(current, AXES, swap_route(FIRST))
-    two = lax.ppermute(current, AXES, swap_route(SECOND))
+    one = near(lax.ppermute(current, AXES, swap_route(FIRST)))
+    two = near(lax.ppermute(current, AXES, swap_route(SECOND)))
     block = call(
         second_product_kernel,
         "second_product",
         [SMEM, SMEM, VMEM, VMEM, VMEM, VMEM, VMEM],
-        shape((T * Z, DW), bf16),
+        pltpu.VMEM((T * Z, DW), bf16),
     )(sizes, partners, block, current, one, two, hinv)
-    block = lax.all_to_all(block, PERIOD, 0, 0, tiled=True)
+    block = near(lax.all_to_all(block, PERIOD, 0, 0, tiled=True))
+    shape = jax.ShapeDtypeStruct
     return call(
         last_sum_kernel, "last_sum", [SMEM, VMEM, VMEM], (shape((Z, 1, V), f32), shape((Z, 1, TIE), f32))
     )(sizes, block, dual)

time: 90.6 us -> 84.9 us (0.937)
  Pallas kernels: 13 us -> 6.39 us
  waiting for transfers between devices: 15.7 us -> 17 us
    pallas_call x2, Pallas kernels: 5.12 us -> 1.65 us  [the longest x1 1.64 us: shards(): call(first_product_kernel, 'first_product', [SMEM, VMEM, VMEM], pltpu.VME...]
    pallas_call x1, Pallas kernels: 4.16 us -> 1.89 us  [shards(): call(second_product_kernel, 'second_product', [SMEM, SMEM, VMEM, VMEM, VM...]
    all_to_all x1, waiting for transfers between devices: 14.3 us -> 15.8 us  [shards(): block = near(lax.all_to_all(block, PERIOD, 0, 0, tiled=True))]
    unnamed x7 -> x15, local copies, waits for them, and re-layouts: 5.04 us -> 5.76 us
  transfers between devices with their start and end apart: 3 -> 3, of which waited for: 2 -> 2; matrix products, arithmetic and copies ran while one was open for 4% -> 2% of each run, Pallas kernels for 0% -> 0%
where the time goes in v2:
time: 84.9 us; the launch traced here: 84.4 us
  blocking collectives  43.9 us (52%)
  waiting for transfers between devices  17 us (20%)
  starting transfers between devices  10.6 us (12%)
  Pallas kernels  6.39 us (8%)
  local copies, waits for them, and re-layouts  5.76 us (7%)
    all_to_all x1, blocking collectives, shards(): block = near(lax.all_to_all(block, PERIOD, 0, 0, tiled=True))  24.9 us
    all_to_all x1, blocking collectives, shards(): ties = near(lax.all_to_all(ties, NEAR, 0, 0, tiled=True))  19 us
    all_to_all x1, waiting for transfers between devices, shards(): block = near(lax.all_to_all(block, PERIOD, 0, 0, tiled=True))  15.8 us
    all_to_all x1, starting transfers between devices, shards(): block = near(lax.all_to_all(block, PERIOD, 0, 0, tiled=True))  8 us
    unnamed x15, local copies, waits for them, and re-layouts  5.76 us
    ppermute x1, starting transfers between devices, shards(): one = near(lax.ppermute(current, AXES, swap_route(FIRST)))  1.92 us
    pallas_call x1, Pallas kernels, shards(): call(second_product_kernel, 'second_product', [SMEM, SMEM, VMEM, VMEM, VM...  1.89 us
  transfers between devices with their start and end apart: 3, of which 2 were waited for; matrix products, arithmetic and copies ran while one was open for 2% of the time, Pallas kernels for 0%

profile of v2, /device:TPU:6, one launch (start us, length us, event | category | flops | bytes accessed | tf_op | source)
XLA Modules:
  0.0 84.4 jit_solution(10306426637676363079)
XLA Ops:
  0.6 0.0 copy-start
  0.6 0.8 copy-done
  1.5 19.0 %all_to_all.33 = f32[16,8,128]{2,1,0:T(8,128)S(1)} all-to-all(f32[16,8,128]{2,1,0:T(8,128)S(1)} %bitcast.11), channel_id=1, replica_groups=mesh['xh'=2,'xl'=2,'zh'=4,'core'=2,'y'=8,'zl'=2] {'xl','zh','core'}, dimensions={0} | all-to-all | bytes 131072 | tf_op jit(solution)/shard_map/all_to_all | solution.py:225
  20.4 0.0 copy-start.1
  20.4 0.8 copy-done.1
  21.2 0.0 copy-start.2
  21.2 0.7 copy-done.2
  22.0 0.0 copy-start.3
  22.0 0.7 copy-done.3
  22.6 0.0 copy-start.5
  22.6 0.7 copy-done.5
  23.3 1.6 %first_side.1 = (bf16[128,2048]{1,0:T(8,128)(2,1)}, f32[8,512]{1,0:T(8,128)S(1)}) custom-call(s32[8]{0:T(128)S(1)} %copy-done.5, s32[4,8]{1,0:T(4,128)S(1)} %copy-done.3, f32[8,1,1600]{2,1,0:T(1,128)S(1)} %copy-done, f32[8,1,512]{2,1,0:T(1,128)S(1)} %copy-done.2, f32[8,1,1600]{2,1,0:T(1,128)S(1)} %copy-done.1, f32[128,128]{1,0:T(8,128)S(1)} %bitcast.10), custom_call_target="tpu_custom_call" | custom-call | tf_op jit(solution)/shard_map/first_side/pallas_call | solution.py:226
  24.9 8.0 %all-to-all-start.1 = ((bf16[16,8,2048]{2,1,0:T(8,128)(2,1)}), bf16[16,8,2048]{2,1,0:T(8,128)(2,1)S(1)}, u32[]{:S(2)}, u32[]{:S(2)}) async-start(bf16[16,8,2048]{2,1,0:T(8,128)(2,1)} %bitcast.2), calls=%async_computation.1 | async-start | bytes 1048576 | tf_op jit(solution)/shard_map/all_to_all | solution.py:232
  32.9 0.0 copy-start.6
  32.9 2.1 %copy.8.hinv_ref = bf16[8,100,1600]{2,1,0:T(8,128)(2,1)S(1)} copy(bf16[8,100,1600]{2,0,1:T(8,128)(2,1)} %param.9) | data formatting | bytes 5120000 | tf_op args[3]
  35.0 0.0 copy-start.4
  35.0 15.8 %all-to-all-done.1 = bf16[16,8,2048]{2,1,0:T(8,128)(2,1)S(1)} async-done(((bf16[16,8,2048]{2,1,0:T(8,128)(2,1)}), bf16[16,8,2048]{2,1,0:T(8,128)(2,1)S(1)}, u32[]{:S(2)}, u32[]{:S(2)}) %all-to-all-start.1) | async-done | bytes 524320 | tf_op jit(solution)/shard_map/all_to_all | solution.py:232
  50.8 0.0 copy-done.6
  50.8 1.6 %first_product.1.current_ref = f32[128,128]{1,0:T(8,128)S(1)} custom-call(s32[8]{0:T(128)S(1)} %copy-done.6, bf16[128,2048]{1,0:T(8,128)(2,1)S(1)} %bitcast.6, bf16[8,100,1600]{2,1,0:T(8,128)(2,1)S(1)} %copy.8.hinv_ref), custom_call_target="tpu_custom_call" | custom-call | tf_op jit(solution)/shard_map/first_product/pallas_call | solution.py:233
  52.5 0.7 collective-permute-start.1
  53.1 1.9 %collective-permute-start = (f32[128,128]{1,0:T(8,128)S(1)}, f32[128,128]{1,0:T(8,128)S(1)}, u32[]{:S(2)}, u32[]{:S(2)}) collective-permute-start(f32[128,128]{1,0:T(8,128)S(1)} %first_product.1.current_ref), channel_id=1, source_target_pairs={{0,16},{1,33},{2,66},{3,67},{4,132},{5,133},{16,0},{17,49},{18,82}... | collective-permute-start | bytes 196616 | tf_op jit(solution)/shard_map/ppermute | solution.py:236
  55.1 0.0 collective-permute-done.1.two_ref
  55.1 1.2 %collective-permute-done.one_ref = f32[128,128]{1,0:T(8,128)S(1)} collective-permute-done((f32[128,128]{1,0:T(8,128)S(1)}, f32[128,128]{1,0:T(8,128)S(1)}, u32[]{:S(2)}, u32[]{:S(2)}) %collective-permute-start) | collective-permute-done | bytes 65568 | tf_op jit(solution)/shard_map/ppermute | solution.py:236
  56.3 0.0 copy-done.4
  56.3 1.9 %second_product.1 = bf16[128,1920]{1,0:T(8,128)(2,1)S(1)} custom-call(s32[8]{0:T(128)S(1)} %copy-done.6, s32[4,8]{1,0:T(4,128)S(1)} %copy-done.4, bf16[128,2048]{1,0:T(8,128)(2,1)S(1)} %bitcast.7, f32[128,128]{1,0:T(8,128)S(1)} %first_product.1.current_ref, f32[128,128]{1,0:T(8,128)S(1)} %collective-permute-done.one_ref, ...), custom_call_target="tpu_custom_call" | custom-call | tf_op jit(solution)/shard_map/second_product/pallas_call | solution.py:238
  58.2 24.9 %all_to_all.34 = bf16[16,8,1920]{2,1,0:T(8,128)(2,1)S(1)} all-to-all(bf16[16,8,1920]{2,1,0:T(8,128)(2,1)S(1)} %bitcast.9), channel_id=1, replica_groups=mesh['xh'=2,'xl'=2,'zh'=4,'core'=2,'y'=8,'zl'=2] {'y','zl'}, dimensions={0} | all-to-all | bytes 983040 | tf_op jit(solution)/shard_map/all_to_all | solution.py:244
  83.1 1.3 %last_sum.1 = (f32[8,1,1600]{2,1,0:T(1,128)}, f32[8,1,512]{2,1,0:T(1,128)}) custom-call(s32[8]{0:T(128)S(1)} %copy-done.6, bf16[128,1920]{1,0:T(8,128)(2,1)S(1)} %bitcast.8, f32[8,512]{1,0:T(8,128)S(1)} %get-tuple-element.5.dual_ref), custom_call_target="tpu_custom_call" | custom-call | tf_op jit(solution)/shard_map/last_sum/pallas_call | solution.py:246
  (1 shorter events, 0.0 us)
Async XLA Ops:
  0.6 0.8 copy-start
  20.4 0.8 copy-start.1
  21.2 0.7 copy-start.2
  22.0 0.7 copy-start.3
  22.6 0.7 copy-start.5
  24.9 25.9 %all-to-all-start.1 = ((bf16[16,8,2048]{2,1,0:T(8,128)(2,1)}), bf16[16,8,2048]{2,1,0:T(8,128)(2,1)S(1)}, u32[]{:S(2)}, u32[]{:S(2)}) async-start(bf16[16,8,2048]{2,1,0:T(8,128)(2,1)} %bitcast.2), calls=%async_computation.1 | async-start | bytes 1048576 | tf_op jit(solution)/shard_map/all_to_all | solution.py:232
  32.9 17.9 %copy-start.6 = (s32[8]{0:T(128)S(1)}, s32[8]{0:T(128)}, u32[]{:S(2)}) copy-start(s32[8]{0:T(128)} %sizes_ref.7) | copy-start | bytes 100
  35.0 21.3 %copy-start.4 = (s32[4,8]{1,0:T(4,128)S(1)}, s32[4,8]{1,0:T(4,128)}, u32[]{:S(2)}) copy-start(s32[4,8]{1,0:T(4,128)} %partners_ref.3) | copy-start | bytes 388
  52.5 2.6 %collective-permute-start.1 = (f32[128,128]{1,0:T(8,128)S(1)}, f32[128,128]{1,0:T(8,128)S(1)}, u32[]{:S(2)}, u32[]{:S(2)}) collective-permute-start(f32[128,128]{1,0:T(8,128)S(1)} %first_product.1.current_ref), channel_id=1, source_target_pairs={{1,17},{2,34},{3,131},{17,1},{18,50},{19,147},{33,49},{34,2},{35,1... | collective-permute-start | bytes 196616 | tf_op jit(solution)/shard_map/ppermute | solution.py:237
  53.1 3.1 %collective-permute-start = (f32[128,128]{1,0:T(8,128)S(1)}, f32[128,128]{1,0:T(8,128)S(1)}, u32[]{:S(2)}, u32[]{:S(2)}) collective-permute-start(f32[128,128]{1,0:T(8,128)S(1)} %first_product.1.current_ref), channel_id=1, source_target_pairs={{0,16},{1,33},{2,66},{3,67},{4,132},{5,133},{16,0},{17,49},{18,82}... | collective-permute-start | bytes 196616 | tf_op jit(solution)/shard_map/ppermute | solution.py:236

commit v3 on v2

v3 whole, which is shorter than its diff:
```python
import itertools

import jax
import jax.numpy as jnp
from jax import lax
from jax.experimental import pallas as pl
from jax.experimental.pallas import tpu as pltpu
from jax.sharding import Mesh, PartitionSpec as P

V = 1600
W = 128
ROUNDS = 4
TIE = ROUNDS * W
RAMP = TIE + W
Z = 8
T = 16
ROWS = V // T
VP = 1664
BW = VP + 3 * W
RP = 104
SIZE_ROW, SIZE_LANE, MATE_ROW = 0, Z, 2 * Z
MATE_LANE = MATE_ROW + ROUNDS * Z
META = MATE_LANE + ROUNDS * Z
DW = VP + 2 * W
AXES = ("xh", "xl", "zh", "core", "y", "zl")
SIZES = (2, 2, 4, 2, 8, 2)
ZONE = ("xh", "xl", "zh", "core")
NEAR = ("xl", "zh", "core")
PERIOD = ("y", "zl")
FIRST = {0: 0, 1: 1, 2: 2, 3: 2, 4: 3, 5: 3}
SECOND = {1: 0, 2: 1, 3: 3}


def near_index():
    return (lax.axis_index("xl") * 4 + lax.axis_index("zh")) * 2 + lax.axis_index("core")


def period_index():
    return lax.axis_index("y") * 2 + lax.axis_index("zl")


def swap_route(rounds):
    route = []
    for place in itertools.product(*[range(size) for size in SIZES]):
        xh, xl, zh, core, y, zl = place
        k = y * 2 + zl
        if k in rounds:
            zone = ((xh * 2 + xl) * 4 + zh) * 2 + core
            mate = zone ^ (1 << rounds[k])
            there = (mate >> 4, (mate >> 3) & 1, (mate >> 1) & 3, mate & 1, y, zl)
            ends = []
            for spot in (place, there):
                flat = 0
                for size, index in zip(SIZES, spot):
                    flat = flat * size + index
                ends.append(flat)
            route.append(tuple(ends))
    return route


def rounded(values):
    return values.astype(jnp.bfloat16)


def two_parts(values):
    high = rounded(values)
    return high, rounded(values - high.astype(jnp.float32))


def fetch_kernel(x_hbm, dual_hbm, cost_hbm, sizes_hbm, partners_hbm, ties_ref, x_ref, dual_ref, cost_ref, meta_ref, sizes_ref, partners_ref, sems):
    pairs = ((x_hbm, x_ref), (sizes_hbm, sizes_ref), (partners_hbm, partners_ref), (dual_hbm, dual_ref), (cost_hbm, cost_ref))
    copies = [pltpu.make_async_copy(here, there, sems.at[i]) for i, (here, there) in enumerate(pairs)]
    for copy in copies:
        copy.start()
    me = near_index()
    ties_ref[...] = jnp.zeros_like(ties_ref)
    row = lax.broadcasted_iota(jnp.int32, (Z, W), 0)
    lane = lax.broadcasted_iota(jnp.int32, (Z, W), 1) & (Z - 1)
    for copy in copies[:3]:
        copy.wait()
    x = x_ref[:, 0, :TIE]
    for r in range(ROUNDS):
        slot = pl.multiple_of((me ^ (1 << r)) * Z, Z)
        ties_ref[pl.ds(slot, Z), :] = x[:, r * W : (r + 1) * W]

    def spread(index, value):
        out = jnp.zeros((Z, W), jnp.int32)
        for z in range(Z):
            out = jnp.where(index == z, value(z), out)
        return out

    meta_ref[SIZE_ROW : SIZE_ROW + Z, :] = spread(row, lambda z: sizes_ref[z])
    meta_ref[SIZE_LANE : SIZE_LANE + Z, :] = spread(lane, lambda z: sizes_ref[z])
    for r in range(ROUNDS):
        at = MATE_ROW + r * Z
        meta_ref[at : at + Z, :] = spread(row, lambda z: partners_ref[r, z])
        at = MATE_LANE + r * Z
        meta_ref[at : at + Z, :] = spread(lane, lambda z: partners_ref[r, z])
    for copy in copies[3:]:
        copy.wait()


def live_rows(meta_ref):
    lane = lax.broadcasted_iota(jnp.int32, (Z, VP), 1)
    size = jnp.concatenate([meta_ref[SIZE_ROW : SIZE_ROW + Z, :]] * (VP // W), axis=1)
    return (lane < size).astype(jnp.float32)[:, :V]


def first_side_kernel(meta_ref, x_ref, dual_ref, cost_ref, ties_ref, hinv_hbm, out_ref, dual_out_ref, hinv_ref, sem):
    fetch = pltpu.make_async_copy(hinv_hbm, hinv_ref, sem)
    fetch.start()
    me = near_index()
    x = x_ref[:, 0, :]
    cost = cost_ref[:, 0, :]
    dual = dual_ref[:, 0, :]
    terms, new_duals = [], []
    for r in range(ROUNDS):
        own = x[:, r * W : (r + 1) * W]
        slot = (me ^ (1 << r)) * Z
        mate = meta_ref[MATE_ROW + r * Z : MATE_ROW + (r + 1) * Z, :]
        other = jnp.zeros((Z, W), jnp.float32)
        for z in range(Z):
            other = jnp.where(mate == z, ties_ref[pl.ds(slot + z, 1), :], other)
        updated = dual[:, r * W : (r + 1) * W] + 0.5 * (own - other)
        new_duals.append(updated)
        terms.append(0.5 * (own + other) - updated)
    new_dual = jnp.concatenate(new_duals, axis=1)
    rest = jnp.zeros((Z, V - TIE), jnp.float32)
    right = (0.5 * x - cost + jnp.concatenate(terms + [rest], axis=1)) * live_rows(meta_ref)
    dual_out_ref[...] = new_dual
    later = cost + jnp.concatenate([new_dual, rest], axis=1)
    later_high, later_low = two_parts(later)
    common = jnp.concatenate(
        [rounded(right), jnp.zeros((Z, VP - V), jnp.bfloat16), rounded(x[:, TIE:RAMP])], axis=1
    )
    blank = jnp.zeros((Z, W - ROWS), jnp.bfloat16)
    for k in range(T):
        own_rows = slice(k * ROWS, (k + 1) * ROWS)
        out_ref[k * Z : (k + 1) * Z, :] = jnp.concatenate(
            [common, later_high[:, own_rows], blank, later_low[:, own_rows], blank], axis=1
        )
    fetch.wait()


def zone_match():
    row = lax.broadcasted_iota(jnp.int32, (Z, T * Z), 0)
    lane = lax.broadcasted_iota(jnp.int32, (Z, T * Z), 1)
    return row == (lane & (Z - 1))


def first_product_kernel(meta_ref, block_ref, hinv_ref, out_ref):
    first = period_index() * ROWS
    ramp = block_ref[:, VP : VP + W].astype(jnp.float32)
    edge = jnp.zeros((Z, W), jnp.float32)
    around = jnp.concatenate([edge, ramp[:-Z]], axis=0) + jnp.concatenate([ramp[Z:], edge], axis=0)
    ramp_side = block_ref[:, TIE:RAMP].astype(jnp.float32) + 0.5 * around
    side = jnp.concatenate([block_ref[:, :TIE], rounded(ramp_side), block_ref[:, RAMP:V]], axis=1)
    product = lax.dot_general(
        hinv_ref[...], side, (((1,), (1,)), ((), ())), preferred_element_type=jnp.float32
    ).reshape(ROWS, Z, T * Z)
    current = jnp.sum(jnp.where(zone_match()[None], product, 0.0), axis=1)
    row = lax.broadcasted_iota(jnp.int32, (ROWS, T * Z), 0) + first
    size = meta_ref[SIZE_LANE : SIZE_LANE + 1, :]
    out_ref[:ROWS, :] = jnp.where(row < size, current, 0.0)
    out_ref[ROWS:, :] = jnp.zeros((RP - ROWS, T * Z), jnp.float32)


def second_product_kernel(meta_ref, block_ref, current_ref, one_ref, two_ref, hinv_ref, out_ref):
    k = period_index()
    first_round = jnp.where(k == 0, 0, jnp.where(k == 1, 1, jnp.where(k <= 3, 2, 3)))
    second_round = jnp.where(k == 1, 0, jnp.where(k == 2, 1, jnp.where(k == 3, 3, 0)))
    current = current_ref[...]
    later = block_ref[:, VP + W : VP + 2 * W].astype(jnp.float32) + block_ref[:, VP + 2 * W :].astype(jnp.float32)
    later = later.T[:RP]
    place = lax.broadcasted_iota(jnp.int32, (T * Z, T * Z), 0)
    group = lax.broadcasted_iota(jnp.int32, (T * Z, T * Z), 1) & ~(Z - 1)

    def pick(round_index):
        mate = meta_ref[pl.ds(MATE_LANE + round_index * Z, 1), :]
        return (place == group + mate).astype(jnp.float32)

    row = lax.broadcasted_iota(jnp.int32, (RP, T * Z), 0)
    lane = lax.broadcasted_iota(jnp.int32, (RP, T * Z), 1)
    entry = row + k * ROWS
    round_of = entry >> 7
    tie = entry < TIE
    received = jnp.concatenate(
        [
            jnp.where(tie & (round_of == first_round), one_ref[...], 0.0),
            jnp.where(tie & (round_of == second_round) & (k >= 1) & (k <= 3), two_ref[...], 0.0),
        ],
        axis=1,
    )
    picks = jnp.concatenate([pick(first_round), pick(second_round)], axis=0)
    other = jnp.dot(received, picks, preferred_element_type=jnp.float32, precision=lax.Precision.HIGHEST)
    before = jnp.where(lane < Z, 0.0, pltpu.roll(current, Z, 1))
    after = jnp.where(lane >= (T - 1) * Z, 0.0, pltpu.roll(current, (T - 1) * Z, 1))
    ramp = jnp.where((entry >= TIE) & (entry < RAMP), 0.5 * (before + after), 0.0)
    right = 0.5 * current - later + jnp.where(tie, other, ramp)
    size = meta_ref[SIZE_LANE : SIZE_LANE + 1, :]
    right = jnp.where(entry < size, right, 0.0)[:ROWS]
    side = rounded(jnp.where(zone_match()[None], right[:, None, :], 0.0).reshape(ROWS * Z, T * Z))
    step = jnp.where(tie, 0.5 * (current - other), 0.0)
    step = jnp.concatenate([step, jnp.zeros((W - RP, T * Z), jnp.float32)], axis=0).T
    step_high, step_low = two_parts(step)
    out_ref[:, VP : VP + W] = step_high
    out_ref[:, VP + W :] = step_low
    total = lax.dot_general(side, hinv_ref[...], (((0,), (0,)), ((), ())), preferred_element_type=jnp.float32)
    out_ref[:, :V] = rounded(total)
    out_ref[:, V:VP] = jnp.zeros((T * Z, VP - V), jnp.bfloat16)


def last_sum_kernel(meta_ref, block_ref, dual_ref, primal_ref, dual_out_ref):
    total = jnp.zeros((Z, V), jnp.float32)
    for k in range(T):
        total = total + block_ref[k * Z : (k + 1) * Z, :V].astype(jnp.float32)
    primal_ref[:, 0, :] = total * live_rows(meta_ref)
    steps = []
    for k in range(-(-TIE // ROWS)):
        part = block_ref[k * Z : (k + 1) * Z, VP : VP + W].astype(jnp.float32) + block_ref[
            k * Z : (k + 1) * Z, VP + W :
        ].astype(jnp.float32)
        steps.append(part[:, : min(ROWS, TIE - k * ROWS)])
    dual_out_ref[:, 0, :] = dual_ref[...] + jnp.concatenate(steps, axis=1)


HBM = pl.BlockSpec(memory_space=pltpu.HBM)
VMEM = pl.BlockSpec(memory_space=pltpu.VMEM)


def call(kernel, name, in_specs, out_shape, scratch=()):
    many = isinstance(out_shape, tuple)
    return pl.pallas_call(
        kernel,
        name=name,
        in_specs=in_specs,
        out_specs=tuple(VMEM for _ in out_shape) if many else VMEM,
        out_shape=out_shape,
        scratch_shapes=scratch,
        compiler_params=pltpu.CompilerParams(vmem_limit_bytes=16 << 20),
    )


def near(values):
    return pltpu.with_memory_space_constraint(values, pltpu.VMEM)


def far(values):
    return pltpu.with_memory_space_constraint(values, pltpu.HBM)


def shards(x, duals, cost, hinv, sizes, partners):
    f32, bf16 = jnp.float32, jnp.bfloat16
    hinv = jnp.transpose(hinv, (1, 0, 2)).reshape(ROWS * Z, V)
    ties, x, duals, cost, meta = call(
        fetch_kernel,
        "fetch",
        [HBM] * 5,
        (
            pltpu.VMEM((T * Z, W), f32),
            pltpu.VMEM((Z, 1, V), f32),
            pltpu.VMEM((Z, 1, TIE), f32),
            pltpu.VMEM((Z, 1, V), f32),
            pltpu.VMEM((META, W), jnp.int32),
        ),
        [pltpu.SMEM((Z,), jnp.int32), pltpu.SMEM((ROUNDS, Z), jnp.int32), pltpu.SemaphoreType.DMA((5,))],
    )(far(x), far(duals), far(cost), far(sizes), far(partners))
    ties = near(lax.all_to_all(ties, NEAR, 0, 0, tiled=True))
    block, dual, hinv = call(
        first_side_kernel,
        "first_side",
        [VMEM] * 5 + [HBM],
        (pltpu.VMEM((T * Z, BW), bf16), pltpu.VMEM((Z, TIE), f32), pltpu.VMEM((ROWS * Z, V), bf16)),
        [pltpu.SemaphoreType.DMA],
    )(meta, x, duals, cost, ties, far(hinv))
    block = near(lax.all_to_all(block, PERIOD, 0, 0, tiled=True))
    current = call(first_product_kernel, "first_product", [VMEM] * 3, pltpu.VMEM((RP, T * Z), f32))(
        meta, block, hinv
    )
    one = near(lax.ppermute(current, AXES, swap_route(FIRST)))
    two = near(lax.ppermute(current, AXES, swap_route(SECOND)))
    block = call(second_product_kernel, "second_product", [VMEM] * 6, pltpu.VMEM((T * Z, DW), bf16))(
        meta, block, current, one, two, hinv
    )
    block = near(lax.all_to_all(block, PERIOD, 0, 0, tiled=True))
    shape = jax.ShapeDtypeStruct
    return call(last_sum_kernel, "last_sum", [VMEM] * 3, (shape((Z, 1, V), f32), shape((Z, 1, TIE), f32)))(
        meta, block, dual
    )


def solution(mesh):
    fine = Mesh(mesh.devices.reshape(SIZES), AXES)
    whole = P(ZONE, PERIOD, None)
    return jax.shard_map(
        shards,
        mesh=fine,
        in_specs=(whole, whole, whole, whole, P(ZONE), P(None, ZONE)),
        out_specs=(whole, whole),
        check_vma=False,
    )
```

time: 84.9 us -> 79.5 us (0.936)
  blocking collectives: 43.9 us -> 69.4 us
  waiting for transfers between devices: 17 us -> 1.19 us
  starting transfers between devices: 10.6 us -> 2.58 us
  local copies, waits for them, and re-layouts: 5.76 us -> 0 us
  Pallas kernels: 6.39 us -> 5.24 us
    all_to_all x1 -> x2, blocking collectives: 24.9 us -> 50.4 us  [shards(): block = near(lax.all_to_all(block, PERIOD, 0, 0, tiled=True))]
    all_to_all x1 -> x0, waiting for transfers between devices: 15.8 us -> none  [shards(): block = near(lax.all_to_all(block, PERIOD, 0, 0, tiled=True))]
    all_to_all x1 -> x0, starting transfers between devices: 8 us -> none  [shards(): block = near(lax.all_to_all(block, PERIOD, 0, 0, tiled=True))]
    unnamed x15 -> x0, local copies, waits for them, and re-layouts: 5.76 us -> none
    pallas_call x5, Pallas kernels: 6.39 us -> 5.24 us  [the longest x1 1.79 us: shards(): call(first_side_kernel, 'first_side', [VMEM] * 5 + [HBM], (pltpu.VMEM((T...]
  transfers between devices with their start and end apart: 3 -> 2, of which waited for: 2 -> 1; matrix products, arithmetic and copies ran while one was open for 2% -> 0% of each run, Pallas kernels for 0% -> 0%
where the time goes in v3:
time: 79.5 us; the launch traced here: 79.1 us
  blocking collectives  69.4 us (87%)
  Pallas kernels  5.24 us (7%)
  starting transfers between devices  2.58 us (3%)
  waiting for transfers between devices  1.19 us (1%)
    all_to_all x2, blocking collectives, shards(): block = near(lax.all_to_all(block, PERIOD, 0, 0, tiled=True))  50.4 us
    all_to_all x1, blocking collectives, shards(): ties = near(lax.all_to_all(ties, NEAR, 0, 0, tiled=True))  19 us
    ppermute x1, starting transfers between devices, shards(): one = near(lax.ppermute(current, AXES, swap_route(FIRST)))  1.92 us
    pallas_call x1, Pallas kernels, shards(): call(first_side_kernel, 'first_side', [VMEM] * 5 + [HBM], (pltpu.VMEM((T...  1.79 us
  transfers between devices with their start and end apart: 2, of which 1 were waited for; matrix products, arithmetic and copies ran while one was open for 0% of the time, Pallas kernels for 0%

profile of v3, /device:TPU:6, one launch (start us, length us, event | category | flops | bytes accessed | tf_op | source)
XLA Modules:
  0.0 79.1 jit_solution(17023619643163371559)
XLA Ops:
  0.6 0.9 %fetch.1 = (f32[128,128]{1,0:T(8,128)S(1)}, f32[8,1,1600]{2,1,0:T(1,128)S(1)}, f32[8,1,512]{2,1,0:T(1,128)S(1)}, f32[8,1,1600]{2,1,0:T(1,128)S(1)}, s32[80,128]{1,0:T(8,128)S(1)}) custom-call(f32[8,1,1600]{2,1,0:T(1,128)} %x_hbm.1, f32[8,1,512]{2,1,0:T(1,128)} %dual_hbm.1, f32[8,1,1600]{2,1,0:T(1,128)} %cost_hbm.1, s32[8]{0:T(128)} %sizes_hbm.1, ...), custom_call_target="tpu_custom_call" | custom-call | tf_op jit(solution)/shard_map/fetch/pallas_call | solution.py:255
  1.5 19.0 %all_to_all.33 = f32[16,8,128]{2,1,0:T(8,128)S(1)} all-to-all(f32[16,8,128]{2,1,0:T(8,128)S(1)} %bitcast.15), channel_id=1, replica_groups=mesh['xh'=2,'xl'=2,'zh'=4,'core'=2,'y'=8,'zl'=2] {'xl','zh','core'}, dimensions={0} | all-to-all | bytes 131072 | tf_op jit(solution)/shard_map/all_to_all | solution.py:268
  20.5 1.8 %first_side.1 = (bf16[128,2048]{1,0:T(8,128)(2,1)S(1)}, f32[8,512]{1,0:T(8,128)S(1)}, bf16[800,1600]{1,0:T(8,128)(2,1)S(1)}) custom-call(s32[80,128]{1,0:T(8,128)S(1)} %get-tuple-element.10.meta_ref, f32[8,1,1600]{2,1,0:T(1,128)S(1)} %get-tuple-element.11.x_ref, f32[8,1,512]{2,1,0:T(1,128)S(1)} %get-tuple-element.12.dual_ref, ...), custom_call_target="tpu_custom_call" | custom-call | tf_op jit(solution)/shard_map/first_side/pallas_call | solution.py:269
  22.3 25.7 %all_to_all.34 = bf16[16,8,2048]{2,1,0:T(8,128)(2,1)S(1)} all-to-all(bf16[16,8,2048]{2,1,0:T(8,128)(2,1)S(1)} %bitcast.13), channel_id=1, replica_groups=mesh['xh'=2,'xl'=2,'zh'=4,'core'=2,'y'=8,'zl'=2] {'y','zl'}, dimensions={0} | all-to-all | bytes 1048576 | tf_op jit(solution)/shard_map/all_to_all | solution.py:276
  48.1 0.9 %first_product.1.current_ref = f32[104,128]{1,0:T(8,128)S(1)} custom-call(s32[80,128]{1,0:T(8,128)S(1)} %get-tuple-element.10.meta_ref, bf16[128,2048]{1,0:T(8,128)(2,1)S(1)} %bitcast.9, bf16[800,1600]{1,0:T(8,128)(2,1)S(1)} %get-tuple-element.16.hinv_ref), custom_call_target="tpu_custom_call" | custom-call | tf_op jit(solution)/shard_map/first_product/pallas_call | solution.py:277
  48.9 0.7 collective-permute-start.1
  49.6 1.9 %collective-permute-start = (f32[104,128]{1,0:T(8,128)S(1)}, f32[104,128]{1,0:T(8,128)S(1)}, u32[]{:S(2)}, u32[]{:S(2)}) collective-permute-start(f32[104,128]{1,0:T(8,128)S(1)} %first_product.1.current_ref), channel_id=1, source_target_pairs={{0,16},{1,33},{2,66},{3,67},{4,132},{5,133},{16,0},{17,49},{18,82}... | collective-permute-start | bytes 159752 | tf_op jit(solution)/shard_map/ppermute | solution.py:280
  51.5 0.0 collective-permute-done.1.two_ref
  51.6 1.2 %collective-permute-done.one_ref = f32[104,128]{1,0:T(8,128)S(1)} collective-permute-done((f32[104,128]{1,0:T(8,128)S(1)}, f32[104,128]{1,0:T(8,128)S(1)}, u32[]{:S(2)}, u32[]{:S(2)}) %collective-permute-start) | collective-permute-done | bytes 53280 | tf_op jit(solution)/shard_map/ppermute | solution.py:280
  52.7 1.0 %second_product.1 = bf16[128,1920]{1,0:T(8,128)(2,1)S(1)} custom-call(s32[80,128]{1,0:T(8,128)S(1)} %get-tuple-element.10.meta_ref, bf16[128,2048]{1,0:T(8,128)(2,1)S(1)} %bitcast.10, f32[104,128]{1,0:T(8,128)S(1)} %first_product.1.current_ref, f32[104,128]{1,0:T(8,128)S(1)} %collective-permute-done.one_ref, f32[104,128]{1,0:T(8,128)S(1)} %collective-permute-done.1.two_ref, ...), custom_call_target="tpu_custom_call" | custom-call | tf_op jit(solution)/shard_map/second_product/pallas_call | solution.py:282
  53.7 24.7 %all_to_all.35 = bf16[16,8,1920]{2,1,0:T(8,128)(2,1)S(1)} all-to-all(bf16[16,8,1920]{2,1,0:T(8,128)(2,1)S(1)} %bitcast.12), channel_id=1, replica_groups=mesh['xh'=2,'xl'=2,'zh'=4,'core'=2,'y'=8,'zl'=2] {'y','zl'}, dimensions={0} | all-to-all | bytes 983040 | tf_op jit(solution)/shard_map/all_to_all | solution.py:285
  78.4 0.7 last_sum.1
Async XLA Ops:
  48.9 2.6 %collective-permute-start.1 = (f32[104,128]{1,0:T(8,128)S(1)}, f32[104,128]{1,0:T(8,128)S(1)}, u32[]{:S(2)}, u32[]{:S(2)}) collective-permute-start(f32[104,128]{1,0:T(8,128)S(1)} %first_product.1.current_ref), channel_id=1, source_target_pairs={{1,17},{2,34},{3,131},{17,1},{18,50},{19,147},{33,49},{34,2},{35,1... | collective-permute-start | bytes 159752 | tf_op jit(solution)/shard_map/ppermute | solution.py:281
  49.6 3.1 %collective-permute-start = (f32[104,128]{1,0:T(8,128)S(1)}, f32[104,128]{1,0:T(8,128)S(1)}, u32[]{:S(2)}, u32[]{:S(2)}) collective-permute-start(f32[104,128]{1,0:T(8,128)S(1)} %first_product.1.current_ref), channel_id=1, source_target_pairs={{0,16},{1,33},{2,66},{3,67},{4,132},{5,133},{16,0},{17,49},{18,82}... | collective-permute-start | bytes 159752 | tf_op jit(solution)/shard_map/ppermute | solution.py:280

commit v4 on v3

--- a/solution.py
+++ b/solution.py
@@ -16,12 +16,15 @@
 T = 16
 ROWS = V // T
 VP = 1664
-BW = VP + 3 * W
+LOW = 92
+TAIL = 1536
+RAMP_AT = V + ROWS + LOW
+BW = RAMP_AT + W
 RP = 104
 SIZE_ROW, SIZE_LANE, MATE_ROW = 0, Z, 2 * Z
 MATE_LANE = MATE_ROW + ROUNDS * Z
 META = MATE_LANE + ROUNDS * Z
-DW = VP + 2 * W
+DW = VP + W
 AXES = ("xh", "xl", "zh", "core", "y", "zl")
 SIZES = (2, 2, 4, 2, 8, 2)
 ZONE = ("xh", "xl", "zh", "core")
@@ -60,11 +63,6 @@
 
 def rounded(values):
     return values.astype(jnp.bfloat16)
-
-
-def two_parts(values):
-    high = rounded(values)
-    return high, rounded(values - high.astype(jnp.float32))
 
 
 def fetch_kernel(x_hbm, dual_hbm, cost_hbm, sizes_hbm, partners_hbm, ties_ref, x_ref, dual_ref, cost_ref, meta_ref, sizes_ref, partners_ref, sems):
@@ -129,15 +127,14 @@
     right = (0.5 * x - cost + jnp.concatenate(terms + [rest], axis=1)) * live_rows(meta_ref)
     dual_out_ref[...] = new_dual
     later = cost + jnp.concatenate([new_dual, rest], axis=1)
-    later_high, later_low = two_parts(later)
-    common = jnp.concatenate(
-        [rounded(right), jnp.zeros((Z, VP - V), jnp.bfloat16), rounded(x[:, TIE:RAMP])], axis=1
-    )
-    blank = jnp.zeros((Z, W - ROWS), jnp.bfloat16)
+    later_high = rounded(later).astype(jnp.float32)
+    later_low = later - later_high
+    head, ramp = rounded(right[:, :TAIL]), rounded(x[:, TIE:RAMP])
     for k in range(T):
-        own_rows = slice(k * ROWS, (k + 1) * ROWS)
+        at = k * ROWS
+        tail = [right[:, TAIL:], later_high[:, at : at + ROWS], later_low[:, at : at + LOW]]
         out_ref[k * Z : (k + 1) * Z, :] = jnp.concatenate(
-            [common, later_high[:, own_rows], blank, later_low[:, own_rows], blank], axis=1
+            [head, rounded(jnp.concatenate(tail, axis=1)), ramp], axis=1
         )
     fetch.wait()
 
@@ -150,7 +147,7 @@
 
 def first_product_kernel(meta_ref, block_ref, hinv_ref, out_ref):
     first = period_index() * ROWS
-    ramp = block_ref[:, VP : VP + W].astype(jnp.float32)
+    ramp = block_ref[:, RAMP_AT:].astype(jnp.float32)
     edge = jnp.zeros((Z, W), jnp.float32)
     around = jnp.concatenate([edge, ramp[:-Z]], axis=0) + jnp.concatenate([ramp[Z:], edge], axis=0)
     ramp_side = block_ref[:, TIE:RAMP].astype(jnp.float32) + 0.5 * around
@@ -165,13 +162,14 @@
     out_ref[ROWS:, :] = jnp.zeros((RP - ROWS, T * Z), jnp.float32)
 
 
-def second_product_kernel(meta_ref, block_ref, current_ref, one_ref, two_ref, hinv_ref, out_ref):
+def second_product_kernel(meta_ref, block_ref, current_ref, two_ref, one_ref, hinv_ref, out_ref):
     k = period_index()
     first_round = jnp.where(k == 0, 0, jnp.where(k == 1, 1, jnp.where(k <= 3, 2, 3)))
     second_round = jnp.where(k == 1, 0, jnp.where(k == 2, 1, jnp.where(k == 3, 3, 0)))
     current = current_ref[...]
-    later = block_ref[:, VP + W : VP + 2 * W].astype(jnp.float32) + block_ref[:, VP + 2 * W :].astype(jnp.float32)
-    later = later.T[:RP]
+    later = block_ref[:, TAIL:RAMP_AT].astype(jnp.float32).T[V - TAIL :]
+    blank = jnp.zeros((RP - LOW, T * Z), jnp.float32)
+    later = jnp.concatenate([later[:ROWS], blank[: RP - ROWS]], axis=0) + jnp.concatenate([later[ROWS:], blank], axis=0)
     place = lax.broadcasted_iota(jnp.int32, (T * Z, T * Z), 0)
     group = lax.broadcasted_iota(jnp.int32, (T * Z, T * Z), 1) & ~(Z - 1)
 
@@ -202,9 +200,7 @@
     side = rounded(jnp.where(zone_match()[None], right[:, None, :], 0.0).reshape(ROWS * Z, T * Z))
     step = jnp.where(tie, 0.5 * (current - other), 0.0)
     step = jnp.concatenate([step, jnp.zeros((W - RP, T * Z), jnp.float32)], axis=0).T
-    step_high, step_low = two_parts(step)
-    out_ref[:, VP : VP + W] = step_high
-    out_ref[:, VP + W :] = step_low
+    out_ref[:, VP:] = rounded(step)
     total = lax.dot_general(side, hinv_ref[...], (((0,), (0,)), ((), ())), preferred_element_type=jnp.float32)
     out_ref[:, :V] = rounded(total)
     out_ref[:, V:VP] = jnp.zeros((T * Z, VP - V), jnp.bfloat16)
@@ -217,9 +213,7 @@
     primal_ref[:, 0, :] = total * live_rows(meta_ref)
     steps = []
     for k in range(-(-TIE // ROWS)):
-        part = block_ref[k * Z : (k + 1) * Z, VP : VP + W].astype(jnp.float32) + block_ref[
-            k * Z : (k + 1) * Z, VP + W :
-        ].astype(jnp.float32)
+        part = block_ref[k * Z : (k + 1) * Z, VP:].astype(jnp.float32)
         steps.append(part[:, : min(ROWS, TIE - k * ROWS)])
     dual_out_ref[:, 0, :] = dual_ref[...] + jnp.concatenate(steps, axis=1)
 
@@ -277,10 +271,10 @@
     current = call(first_product_kernel, "first_product", [VMEM] * 3, pltpu.VMEM((RP, T * Z), f32))(
         meta, block, hinv
     )
+    two = near(lax.ppermute(current, AXES, swap_route(SECOND)))
     one = near(lax.ppermute(current, AXES, swap_route(FIRST)))
-    two = near(lax.ppermute(current, AXES, swap_route(SECOND)))
     block = call(second_product_kernel, "second_product", [VMEM] * 6, pltpu.VMEM((T * Z, DW), bf16))(
-        meta, block, current, one, two, hinv
+        meta, block, current, two, one, hinv
     )
     block = near(lax.all_to_all(block, PERIOD, 0, 0, tiled=True))
     shape = jax.ShapeDtypeStruct

time: 79.5 us -> 76 us (0.956)
  blocking collectives: 69.4 us -> 65.8 us
    all_to_all x2, blocking collectives: 50.4 us -> 46.8 us  [shards(): block = near(lax.all_to_all(block, PERIOD, 0, 0, tiled=True))]
where the time goes in v4:
time: 76 us; the launch traced here: 74.9 us
  blocking collectives  65.8 us (87%)
  Pallas kernels  5.3 us (7%)
  starting transfers between devices  2.58 us (3%)
    all_to_all x2, blocking collectives, shards(): block = near(lax.all_to_all(block, PERIOD, 0, 0, tiled=True))  46.8 us
    all_to_all x1, blocking collectives, shards(): ties = near(lax.all_to_all(ties, NEAR, 0, 0, tiled=True))  19 us
    ppermute x1, starting transfers between devices, shards(): one = near(lax.ppermute(current, AXES, swap_route(FIRST)))  1.92 us
    pallas_call x1, Pallas kernels, shards(): call(first_side_kernel, 'first_side', [VMEM] * 5 + [HBM], (pltpu.VMEM((T...  1.84 us
  transfers between devices with their start and end apart: 2, of which 1 were waited for; matrix products, arithmetic and copies ran while one was open for 0% of the time, Pallas kernels for 0%

profile of v4, /device:TPU:6, one launch (start us, length us, event | category | flops | bytes accessed | tf_op | source)
XLA Modules:
  0.0 74.9 jit_solution(8481883587316553296)
XLA Ops:
  0.6 0.9 %fetch.1 = (f32[128,128]{1,0:T(8,128)S(1)}, f32[8,1,1600]{2,1,0:T(1,128)S(1)}, f32[8,1,512]{2,1,0:T(1,128)S(1)}, f32[8,1,1600]{2,1,0:T(1,128)S(1)}, s32[80,128]{1,0:T(8,128)S(1)}) custom-call(f32[8,1,1600]{2,1,0:T(1,128)} %x_hbm.1, f32[8,1,512]{2,1,0:T(1,128)} %dual_hbm.1, f32[8,1,1600]{2,1,0:T(1,128)} %cost_hbm.1, s32[8]{0:T(128)} %sizes_hbm.1, ...), custom_call_target="tpu_custom_call" | custom-call | tf_op jit(solution)/shard_map/fetch/pallas_call | solution.py:249
  1.5 19.0 %all_to_all.33 = f32[16,8,128]{2,1,0:T(8,128)S(1)} all-to-all(f32[16,8,128]{2,1,0:T(8,128)S(1)} %bitcast.15), channel_id=1, replica_groups=mesh['xh'=2,'xl'=2,'zh'=4,'core'=2,'y'=8,'zl'=2] {'xl','zh','core'}, dimensions={0} | all-to-all | bytes 131072 | tf_op jit(solution)/shard_map/all_to_all | solution.py:262
  20.5 1.8 %first_side.1 = (bf16[128,1920]{1,0:T(8,128)(2,1)S(1)}, f32[8,512]{1,0:T(8,128)S(1)}, bf16[800,1600]{1,0:T(8,128)(2,1)S(1)}) custom-call(s32[80,128]{1,0:T(8,128)S(1)} %get-tuple-element.10.meta_ref, f32[8,1,1600]{2,1,0:T(1,128)S(1)} %get-tuple-element.11.x_ref, f32[8,1,512]{2,1,0:T(1,128)S(1)} %get-tuple-element.12.dual_ref, ...), custom_call_target="tpu_custom_call" | custom-call | tf_op jit(solution)/shard_map/first_side/pallas_call | solution.py:263
  22.4 25.1 %all_to_all.34 = bf16[16,8,1920]{2,1,0:T(8,128)(2,1)S(1)} all-to-all(bf16[16,8,1920]{2,1,0:T(8,128)(2,1)S(1)} %bitcast.13), channel_id=1, replica_groups=mesh['xh'=2,'xl'=2,'zh'=4,'core'=2,'y'=8,'zl'=2] {'y','zl'}, dimensions={0} | all-to-all | bytes 983040 | tf_op jit(solution)/shard_map/all_to_all | solution.py:270
  47.4 0.9 %first_product.1.current_ref = f32[104,128]{1,0:T(8,128)S(1)} custom-call(s32[80,128]{1,0:T(8,128)S(1)} %get-tuple-element.10.meta_ref, bf16[128,1920]{1,0:T(8,128)(2,1)S(1)} %bitcast.9, bf16[800,1600]{1,0:T(8,128)(2,1)S(1)} %get-tuple-element.16.hinv_ref), custom_call_target="tpu_custom_call" | custom-call | tf_op jit(solution)/shard_map/first_product/pallas_call | solution.py:271
  48.3 1.9 %collective-permute-start.1 = (f32[104,128]{1,0:T(8,128)S(1)}, f32[104,128]{1,0:T(8,128)S(1)}, u32[]{:S(2)}, u32[]{:S(2)}) collective-permute-start(f32[104,128]{1,0:T(8,128)S(1)} %first_product.1.current_ref), channel_id=1, source_target_pairs={{0,16},{1,33},{2,66},{3,67},{4,132},{5,133},{16,0},{17,49},{18,82}... | collective-permute-start | bytes 159752 | tf_op jit(solution)/shard_map/ppermute | solution.py:275
  50.2 0.7 collective-permute-start
  50.9 0.5 collective-permute-done.1.one_ref
  51.4 0.0 collective-permute-done.two_ref
  51.4 1.0 %second_product.1 = bf16[128,1792]{1,0:T(8,128)(2,1)S(1)} custom-call(s32[80,128]{1,0:T(8,128)S(1)} %get-tuple-element.10.meta_ref, bf16[128,1920]{1,0:T(8,128)(2,1)S(1)} %bitcast.10, f32[104,128]{1,0:T(8,128)S(1)} %first_product.1.current_ref, f32[104,128]{1,0:T(8,128)S(1)} %collective-permute-done.two_ref, f32[104,128]{1,0:T(8,128)S(1)} %collective-permute-done.1.one_ref, ...), custom_call_target="tpu_custom_call" | custom-call | tf_op jit(solution)/shard_map/second_product/pallas_call | solution.py:276
  52.4 21.8 %all_to_all.35 = bf16[16,8,1792]{2,1,0:T(8,128)(2,1)S(1)} all-to-all(bf16[16,8,1792]{2,1,0:T(8,128)(2,1)S(1)} %bitcast.12), channel_id=1, replica_groups=mesh['xh'=2,'xl'=2,'zh'=4,'core'=2,'y'=8,'zl'=2] {'y','zl'}, dimensions={0} | all-to-all | bytes 917504 | tf_op jit(solution)/shard_map/all_to_all | solution.py:279
  74.2 0.7 last_sum.1
Async XLA Ops:
  48.3 3.1 %collective-permute-start.1 = (f32[104,128]{1,0:T(8,128)S(1)}, f32[104,128]{1,0:T(8,128)S(1)}, u32[]{:S(2)}, u32[]{:S(2)}) collective-permute-start(f32[104,128]{1,0:T(8,128)S(1)} %first_product.1.current_ref), channel_id=1, source_target_pairs={{0,16},{1,33},{2,66},{3,67},{4,132},{5,133},{16,0},{17,49},{18,82}... | collective-permute-start | bytes 159752 | tf_op jit(solution)/shard_map/ppermute | solution.py:275
  50.2 1.2 %collective-permute-start = (f32[104,128]{1,0:T(8,128)S(1)}, f32[104,128]{1,0:T(8,128)S(1)}, u32[]{:S(2)}, u32[]{:S(2)}) collective-permute-start(f32[104,128]{1,0:T(8,128)S(1)} %first_product.1.current_ref), channel_id=1, source_target_pairs={{1,17},{2,34},{3,131},{17,1},{18,50},{19,147},{33,49},{34,2},{35,1... | collective-permute-start | bytes 159752 | tf_op jit(solution)/shard_map/ppermute | solution.py:274

commit v5 on v4

--- a/solution.py
+++ b/solution.py
@@ -30,6 +30,10 @@
 ZONE = ("xh", "xl", "zh", "core")
 NEAR = ("xl", "zh", "core")
 PERIOD = ("y", "zl")
+SLOTS = ("zl", "y")
+ORDER = tuple(range(0, T, 2)) + tuple(range(1, T, 2))
+HALF = T * Z // 2
+SECOND_ROWS = 56
 FIRST = {0: 0, 1: 1, 2: 2, 3: 2, 4: 3, 5: 3}
 SECOND = {1: 0, 2: 1, 3: 3}
 
@@ -130,10 +134,10 @@
     later_high = rounded(later).astype(jnp.float32)
     later_low = later - later_high
     head, ramp = rounded(right[:, :TAIL]), rounded(x[:, TIE:RAMP])
-    for k in range(T):
+    for slot, k in enumerate(ORDER):
         at = k * ROWS
         tail = [right[:, TAIL:], later_high[:, at : at + ROWS], later_low[:, at : at + LOW]]
-        out_ref[k * Z : (k + 1) * Z, :] = jnp.concatenate(
+        out_ref[slot * Z : (slot + 1) * Z, :] = jnp.concatenate(
             [head, rounded(jnp.concatenate(tail, axis=1)), ramp], axis=1
         )
     fetch.wait()
@@ -145,11 +149,18 @@
     return row == (lane & (Z - 1))
 
 
-def first_product_kernel(meta_ref, block_ref, hinv_ref, out_ref):
+def first_product_kernel(meta_ref, block_ref, hinv_ref, out_ref, second_ref):
     first = period_index() * ROWS
     ramp = block_ref[:, RAMP_AT:].astype(jnp.float32)
     edge = jnp.zeros((Z, W), jnp.float32)
-    around = jnp.concatenate([edge, ramp[:-Z]], axis=0) + jnp.concatenate([ramp[Z:], edge], axis=0)
+    even, odd = ramp[:HALF], ramp[HALF:]
+    around = jnp.concatenate(
+        [
+            odd + jnp.concatenate([edge, odd[:-Z]], axis=0),
+            even + jnp.concatenate([even[Z:], edge], axis=0),
+        ],
+        axis=0,
+    )
     ramp_side = block_ref[:, TIE:RAMP].astype(jnp.float32) + 0.5 * around
     side = jnp.concatenate([block_ref[:, :TIE], rounded(ramp_side), block_ref[:, RAMP:V]], axis=1)
     product = lax.dot_general(
@@ -158,8 +169,10 @@
     current = jnp.sum(jnp.where(zone_match()[None], product, 0.0), axis=1)
     row = lax.broadcasted_iota(jnp.int32, (ROWS, T * Z), 0) + first
     size = meta_ref[SIZE_LANE : SIZE_LANE + 1, :]
-    out_ref[:ROWS, :] = jnp.where(row < size, current, 0.0)
-    out_ref[ROWS:, :] = jnp.zeros((RP - ROWS, T * Z), jnp.float32)
+    current = jnp.where(row < size, current, 0.0)
+    current = jnp.concatenate([current, jnp.zeros((RP - ROWS, T * Z), jnp.float32)], axis=0)
+    out_ref[...] = current
+    second_ref[...] = jnp.where(period_index() == 3, current[RP - SECOND_ROWS :], current[:SECOND_ROWS])
 
 
 def second_product_kernel(meta_ref, block_ref, current_ref, two_ref, one_ref, hinv_ref, out_ref):
@@ -182,18 +195,25 @@
     entry = row + k * ROWS
     round_of = entry >> 7
     tie = entry < TIE
+    blank = jnp.zeros((RP - SECOND_ROWS, T * Z), jnp.float32)
+    second = jnp.where(
+        k == 3,
+        jnp.concatenate([blank, two_ref[...]], axis=0),
+        jnp.concatenate([two_ref[...], blank], axis=0),
+    )
     received = jnp.concatenate(
         [
             jnp.where(tie & (round_of == first_round), one_ref[...], 0.0),
-            jnp.where(tie & (round_of == second_round) & (k >= 1) & (k <= 3), two_ref[...], 0.0),
+            jnp.where(tie & (round_of == second_round) & (k >= 1) & (k <= 3), second, 0.0),
         ],
         axis=1,
     )
     picks = jnp.concatenate([pick(first_round), pick(second_round)], axis=0)
     other = jnp.dot(received, picks, preferred_element_type=jnp.float32, precision=lax.Precision.HIGHEST)
-    before = jnp.where(lane < Z, 0.0, pltpu.roll(current, Z, 1))
-    after = jnp.where(lane >= (T - 1) * Z, 0.0, pltpu.roll(current, (T - 1) * Z, 1))
-    ramp = jnp.where((entry >= TIE) & (entry < RAMP), 0.5 * (before + after), 0.0)
+    beside = pltpu.roll(current, HALF, 1)
+    before = jnp.where(lane < Z, 0.0, pltpu.roll(beside, Z, 1))
+    after = jnp.where(lane >= (T - 1) * Z, 0.0, pltpu.roll(beside, (T - 1) * Z, 1))
+    ramp = jnp.where((entry >= TIE) & (entry < RAMP), 0.5 * (beside + jnp.where(lane < HALF, before, after)), 0.0)
     right = 0.5 * current - later + jnp.where(tie, other, ramp)
     size = meta_ref[SIZE_LANE : SIZE_LANE + 1, :]
     right = jnp.where(entry < size, right, 0.0)[:ROWS]
@@ -213,7 +233,8 @@
     primal_ref[:, 0, :] = total * live_rows(meta_ref)
     steps = []
     for k in range(-(-TIE // ROWS)):
-        part = block_ref[k * Z : (k + 1) * Z, VP:].astype(jnp.float32)
+        slot = ORDER.index(k)
+        part = block_ref[slot * Z : (slot + 1) * Z, VP:].astype(jnp.float32)
         steps.append(part[:, : min(ROWS, TIE - k * ROWS)])
     dual_out_ref[:, 0, :] = dual_ref[...] + jnp.concatenate(steps, axis=1)
 
@@ -267,16 +288,19 @@
         (pltpu.VMEM((T * Z, BW), bf16), pltpu.VMEM((Z, TIE), f32), pltpu.VMEM((ROWS * Z, V), bf16)),
         [pltpu.SemaphoreType.DMA],
     )(meta, x, duals, cost, ties, far(hinv))
-    block = near(lax.all_to_all(block, PERIOD, 0, 0, tiled=True))
-    current = call(first_product_kernel, "first_product", [VMEM] * 3, pltpu.VMEM((RP, T * Z), f32))(
-        meta, block, hinv
-    )
-    two = near(lax.ppermute(current, AXES, swap_route(SECOND)))
+    block = near(lax.all_to_all(block, SLOTS, 0, 0, tiled=True))
+    current, part = call(
+        first_product_kernel,
+        "first_product",
+        [VMEM] * 3,
+        (pltpu.VMEM((RP, T * Z), f32), pltpu.VMEM((SECOND_ROWS, T * Z), f32)),
+    )(meta, block, hinv)
+    two = near(lax.ppermute(part, AXES, swap_route(SECOND)))
     one = near(lax.ppermute(current, AXES, swap_route(FIRST)))
     block = call(second_product_kernel, "second_product", [VMEM] * 6, pltpu.VMEM((T * Z, DW), bf16))(
         meta, block, current, two, one, hinv
     )
-    block = near(lax.all_to_all(block, PERIOD, 0, 0, tiled=True))
+    block = near(lax.all_to_all(block, SLOTS, 0, 0, tiled=True))
     shape = jax.ShapeDtypeStruct
     return call(last_sum_kernel, "last_sum", [VMEM] * 3, (shape((Z, 1, V), f32), shape((Z, 1, TIE), f32)))(
         meta, block, dual

time: 76 us -> 75 us (0.987)
  blocking collectives: 65.8 us -> 65 us
    all_to_all x2, blocking collectives: 46.8 us -> 46 us  [shards(): block = near(lax.all_to_all(block, SLOTS, 0, 0, tiled=True))]
where the time goes in v5:
time: 75 us; the launch traced here: 74.2 us
  blocking collectives  65 us (87%)
  Pallas kernels  5.37 us (7%)
  starting transfers between devices  2.58 us (3%)
    all_to_all x2, blocking collectives, shards(): block = near(lax.all_to_all(block, SLOTS, 0, 0, tiled=True))  46 us
    all_to_all x1, blocking collectives, shards(): ties = near(lax.all_to_all(ties, NEAR, 0, 0, tiled=True))  19 us
    ppermute x1, starting transfers between devices, shards(): one = near(lax.ppermute(current, AXES, swap_route(FIRST)))  1.92 us
    pallas_call x1, Pallas kernels, shards(): call(first_side_kernel, 'first_side', [VMEM] * 5 + [HBM], (pltpu.VMEM((T...  1.84 us
  transfers between devices with their start and end apart: 2, of which 1 were waited for; matrix products, arithmetic and copies ran while one was open for 0% of the time, Pallas kernels for 0%

profile of v5, /device:TPU:6, one launch (start us, length us, event | category | flops | bytes accessed | tf_op | source)
XLA Modules:
  0.0 74.2 jit_solution(5330359551468350326)
XLA Ops:
  0.6 0.9 %fetch.1 = (f32[128,128]{1,0:T(8,128)S(1)}, f32[8,1,1600]{2,1,0:T(1,128)S(1)}, f32[8,1,512]{2,1,0:T(1,128)S(1)}, f32[8,1,1600]{2,1,0:T(1,128)S(1)}, s32[80,128]{1,0:T(8,128)S(1)}) custom-call(f32[8,1,1600]{2,1,0:T(1,128)} %x_hbm.1, f32[8,1,512]{2,1,0:T(1,128)} %dual_hbm.1, f32[8,1,1600]{2,1,0:T(1,128)} %cost_hbm.1, s32[8]{0:T(128)} %sizes_hbm.1, ...), custom_call_target="tpu_custom_call" | custom-call | tf_op jit(solution)/shard_map/fetch/pallas_call | solution.py:270
  1.5 19.0 %all_to_all.33 = f32[16,8,128]{2,1,0:T(8,128)S(1)} all-to-all(f32[16,8,128]{2,1,0:T(8,128)S(1)} %bitcast.15), channel_id=1, replica_groups=mesh['xh'=2,'xl'=2,'zh'=4,'core'=2,'y'=8,'zl'=2] {'xl','zh','core'}, dimensions={0} | all-to-all | bytes 131072 | tf_op jit(solution)/shard_map/all_to_all | solution.py:283
  20.5 1.8 %first_side.1 = (bf16[128,1920]{1,0:T(8,128)(2,1)S(1)}, f32[8,512]{1,0:T(8,128)S(1)}, bf16[800,1600]{1,0:T(8,128)(2,1)S(1)}) custom-call(s32[80,128]{1,0:T(8,128)S(1)} %get-tuple-element.12.meta_ref, f32[8,1,1600]{2,1,0:T(1,128)S(1)} %get-tuple-element.13.x_ref, f32[8,1,512]{2,1,0:T(1,128)S(1)} %get-tuple-element.14.dual_ref, ...), custom_call_target="tpu_custom_call" | custom-call | tf_op jit(solution)/shard_map/first_side/pallas_call | solution.py:284
  22.4 22.9 %all_to_all.34 = bf16[16,8,1920]{2,1,0:T(8,128)(2,1)S(1)} all-to-all(bf16[16,8,1920]{2,1,0:T(8,128)(2,1)S(1)} %bitcast.13), channel_id=1, replica_groups=mesh['xh'=2,'xl'=2,'zh'=4,'core'=2,'y'=8,'zl'=2] {'zl','y'}, dimensions={0} | all-to-all | bytes 983040 | tf_op jit(solution)/shard_map/all_to_all | solution.py:291
  45.3 0.9 %first_product.1 = (f32[104,128]{1,0:T(8,128)S(1)}, f32[56,128]{1,0:T(8,128)S(1)}) custom-call(s32[80,128]{1,0:T(8,128)S(1)} %get-tuple-element.12.meta_ref, bf16[128,1920]{1,0:T(8,128)(2,1)S(1)} %bitcast.9, bf16[800,1600]{1,0:T(8,128)(2,1)S(1)} %get-tuple-element.18.hinv_ref), custom_call_target="tpu_custom_call" | custom-call | tf_op jit(solution)/shard_map/first_product/pallas_call | solution.py:292
  46.2 1.9 %collective-permute-start.1 = (f32[104,128]{1,0:T(8,128)S(1)}, f32[104,128]{1,0:T(8,128)S(1)}, u32[]{:S(2)}, u32[]{:S(2)}) collective-permute-start(f32[104,128]{1,0:T(8,128)S(1)} %get-tuple-element.19.current_ref), channel_id=1, source_target_pairs={{0,16},{1,33},{2,66},{3,67},{4,132},{5,133},{16,0},{17,49},{18,82}... | collective-permute-start | bytes 159752 | tf_op jit(solution)/shard_map/ppermute | solution.py:299
  48.1 0.7 collective-permute-start
  48.8 0.0 collective-permute-done.two_ref
  48.8 0.5 collective-permute-done.1.one_ref
  49.3 1.0 %second_product.1 = bf16[128,1792]{1,0:T(8,128)(2,1)S(1)} custom-call(s32[80,128]{1,0:T(8,128)S(1)} %get-tuple-element.12.meta_ref, bf16[128,1920]{1,0:T(8,128)(2,1)S(1)} %bitcast.10, f32[104,128]{1,0:T(8,128)S(1)} %get-tuple-element.19.current_ref, f32[56,128]{1,0:T(8,128)S(1)} %collective-permute-done.two_ref, ...), custom_call_target="tpu_custom_call" | custom-call | tf_op jit(solution)/shard_map/second_product/pallas_call | solution.py:300
  50.3 23.2 %all_to_all.35 = bf16[16,8,1792]{2,1,0:T(8,128)(2,1)S(1)} all-to-all(bf16[16,8,1792]{2,1,0:T(8,128)(2,1)S(1)} %bitcast.12), channel_id=1, replica_groups=mesh['xh'=2,'xl'=2,'zh'=4,'core'=2,'y'=8,'zl'=2] {'zl','y'}, dimensions={0} | all-to-all | bytes 917504 | tf_op jit(solution)/shard_map/all_to_all | solution.py:303
  73.5 0.7 last_sum.1
Async XLA Ops:
  46.2 3.1 %collective-permute-start.1 = (f32[104,128]{1,0:T(8,128)S(1)}, f32[104,128]{1,0:T(8,128)S(1)}, u32[]{:S(2)}, u32[]{:S(2)}) collective-permute-start(f32[104,128]{1,0:T(8,128)S(1)} %get-tuple-element.19.current_ref), channel_id=1, source_target_pairs={{0,16},{1,33},{2,66},{3,67},{4,132},{5,133},{16,0},{17,49},{18,82}... | collective-permute-start | bytes 159752 | tf_op jit(solution)/shard_map/ppermute | solution.py:299
  48.1 0.7 collective-permute-start

commit v6 on v5

--- a/solution.py
+++ b/solution.py
@@ -69,21 +69,39 @@
     return values.astype(jnp.bfloat16)
 
 
-def fetch_kernel(x_hbm, dual_hbm, cost_hbm, sizes_hbm, partners_hbm, ties_ref, x_ref, dual_ref, cost_ref, meta_ref, sizes_ref, partners_ref, sems):
-    pairs = ((x_hbm, x_ref), (sizes_hbm, sizes_ref), (partners_hbm, partners_ref), (dual_hbm, dual_ref), (cost_hbm, cost_ref))
+def tie_blocks_kernel(x_hbm, ties_hbm, blocks_ref, sems, out_sems):
+    me = near_index()
+    copies = []
+    for r in range(ROUNDS):
+        here = x_hbm.at[:, 0, r * W : (r + 1) * W]
+        copies.append(pltpu.make_async_copy(here, blocks_ref.at[r], sems.at[r]))
+        copies[-1].start()
+    sends = []
+    for r in range(ROUNDS):
+        slot = pl.multiple_of((me ^ (1 << r)) * Z, Z)
+        copies[r].wait()
+        sends.append(pltpu.make_async_copy(blocks_ref.at[r], ties_hbm.at[pl.ds(slot, Z), :], out_sems.at[r]))
+        sends[-1].start()
+    for send in sends:
+        send.wait()
+
+
+def fetch_kernel(x_hbm, dual_hbm, cost_hbm, sizes_hbm, partners_hbm, hinv_hbm, x_ref, dual_ref, cost_ref, meta_ref, hinv_ref, sizes_ref, partners_ref, sems):
+    pairs = (
+        (sizes_hbm, sizes_ref),
+        (partners_hbm, partners_ref),
+        (x_hbm, x_ref),
+        (dual_hbm, dual_ref),
+        (cost_hbm, cost_ref),
+        (hinv_hbm, hinv_ref),
+    )
     copies = [pltpu.make_async_copy(here, there, sems.at[i]) for i, (here, there) in enumerate(pairs)]
     for copy in copies:
         copy.start()
-    me = near_index()
-    ties_ref[...] = jnp.zeros_like(ties_ref)
     row = lax.broadcasted_iota(jnp.int32, (Z, W), 0)
     lane = lax.broadcasted_iota(jnp.int32, (Z, W), 1) & (Z - 1)
-    for copy in copies[:3]:
+    for copy in copies[:2]:
         copy.wait()
-    x = x_ref[:, 0, :TIE]
-    for r in range(ROUNDS):
-        slot = pl.multiple_of((me ^ (1 << r)) * Z, Z)
-        ties_ref[pl.ds(slot, Z), :] = x[:, r * W : (r + 1) * W]
 
     def spread(index, value):
         out = jnp.zeros((Z, W), jnp.int32)
@@ -98,7 +116,7 @@
         meta_ref[at : at + Z, :] = spread(row, lambda z: partners_ref[r, z])
         at = MATE_LANE + r * Z
         meta_ref[at : at + Z, :] = spread(lane, lambda z: partners_ref[r, z])
-    for copy in copies[3:]:
+    for copy in copies[2:]:
         copy.wait()
 
 
@@ -108,9 +126,7 @@
     return (lane < size).astype(jnp.float32)[:, :V]
 
 
-def first_side_kernel(meta_ref, x_ref, dual_ref, cost_ref, ties_ref, hinv_hbm, out_ref, dual_out_ref, hinv_ref, sem):
-    fetch = pltpu.make_async_copy(hinv_hbm, hinv_ref, sem)
-    fetch.start()
+def first_side_kernel(meta_ref, x_ref, dual_ref, cost_ref, ties_ref, out_ref, dual_out_ref):
     me = near_index()
     x = x_ref[:, 0, :]
     cost = cost_ref[:, 0, :]
@@ -140,7 +156,6 @@
         out_ref[slot * Z : (slot + 1) * Z, :] = jnp.concatenate(
             [head, rounded(jnp.concatenate(tail, axis=1)), ramp], axis=1
         )
-    fetch.wait()
 
 
 def zone_match():
@@ -243,13 +258,13 @@
 VMEM = pl.BlockSpec(memory_space=pltpu.VMEM)
 
 
-def call(kernel, name, in_specs, out_shape, scratch=()):
+def call(kernel, name, in_specs, out_shape, scratch=(), out_spec=VMEM):
     many = isinstance(out_shape, tuple)
     return pl.pallas_call(
         kernel,
         name=name,
         in_specs=in_specs,
-        out_specs=tuple(VMEM for _ in out_shape) if many else VMEM,
+        out_specs=tuple(out_spec for _ in out_shape) if many else out_spec,
         out_shape=out_shape,
         scratch_shapes=scratch,
         compiler_params=pltpu.CompilerParams(vmem_limit_bytes=16 << 20),
@@ -267,27 +282,34 @@
 def shards(x, duals, cost, hinv, sizes, partners):
     f32, bf16 = jnp.float32, jnp.bfloat16
     hinv = jnp.transpose(hinv, (1, 0, 2)).reshape(ROWS * Z, V)
-    ties, x, duals, cost, meta = call(
+    ties = call(
+        tie_blocks_kernel,
+        "tie_blocks",
+        [HBM],
+        pltpu.HBM((T * Z, W), f32),
+        [pltpu.VMEM((ROUNDS, Z, W), f32)] + [pltpu.SemaphoreType.DMA((ROUNDS,))] * 2,
+        HBM,
+    )(far(x))
+    ties = near(lax.all_to_all(ties, NEAR, 0, 0, tiled=True))
+    x, duals, cost, meta, hinv = call(
         fetch_kernel,
         "fetch",
-        [HBM] * 5,
+        [HBM] * 6,
         (
-            pltpu.VMEM((T * Z, W), f32),
             pltpu.VMEM((Z, 1, V), f32),
             pltpu.VMEM((Z, 1, TIE), f32),
             pltpu.VMEM((Z, 1, V), f32),
             pltpu.VMEM((META, W), jnp.int32),
+            pltpu.VMEM((ROWS * Z, V), bf16),
         ),
-        [pltpu.SMEM((Z,), jnp.int32), pltpu.SMEM((ROUNDS, Z), jnp.int32), pltpu.SemaphoreType.DMA((5,))],
-    )(far(x), far(duals), far(cost), far(sizes), far(partners))
-    ties = near(lax.all_to_all(ties, NEAR, 0, 0, tiled=True))
-    block, dual, hinv = call(
+        [pltpu.SMEM((Z,), jnp.int32), pltpu.SMEM((ROUNDS, Z), jnp.int32), pltpu.SemaphoreType.DMA((6,))],
+    )(far(x), far(duals), far(cost), far(sizes), far(partners), far(hinv))
+    block, dual = call(
         first_side_kernel,
         "first_side",
-        [VMEM] * 5 + [HBM],
-        (pltpu.VMEM((T * Z, BW), bf16), pltpu.VMEM((Z, TIE), f32), pltpu.VMEM((ROWS * Z, V), bf16)),
-        [pltpu.SemaphoreType.DMA],
-    )(meta, x, duals, cost, ties, far(hinv))
+        [VMEM] * 5,
+        (pltpu.VMEM((T * Z, BW), bf16), pltpu.VMEM((Z, TIE), f32)),
+    )(meta, x, duals, cost, ties)
     block = near(lax.all_to_all(block, SLOTS, 0, 0, tiled=True))
     current, part = call(
         first_product_kernel,

time: 75 us -> 74.1 us (0.988)
  blocking collectives: 65 us -> 46.1 us
  starting transfers between devices: 2.58 us -> 14.4 us
  waiting for transfers between devices: 0.52 us -> 6.03 us
    all_to_all x1 -> x0, blocking collectives: 19 us -> none  [shards(): ties = near(lax.all_to_all(ties, NEAR, 0, 0, tiled=True))]
    all_to_all x0 -> x1, starting transfers between devices: none -> 11.8 us  [shards(): ties = near(lax.all_to_all(ties, NEAR, 0, 0, tiled=True))]
    all_to_all x0 -> x1, waiting for transfers between devices: none -> 5.51 us  [shards(): ties = near(lax.all_to_all(ties, NEAR, 0, 0, tiled=True))]
    pallas_call x2 -> x3, Pallas kernels: 2.74 us -> 3.44 us  [the longest x1 1.89 us: shards(): call(fetch_kernel, 'fetch', [HBM] * 6, (pltpu.VMEM((Z, 1, V), f32), pltpu...]
  transfers between devices with their start and end apart: 2 -> 3, of which waited for: 1 -> 2; matrix products, arithmetic and copies ran while one was open for 0% -> 0% of each run, Pallas kernels for 0% -> 3%
where the time goes in v6:
time: 74.1 us; the launch traced here: 73.2 us
  blocking collectives  46.1 us (62%)
  starting transfers between devices  14.4 us (19%)
  Pallas kernels  6.06 us (8%)
  waiting for transfers between devices  6.03 us (8%)
    all_to_all x2, blocking collectives, shards(): block = near(lax.all_to_all(block, SLOTS, 0, 0, tiled=True))  46.1 us
    all_to_all x1, starting transfers between devices, shards(): ties = near(lax.all_to_all(ties, NEAR, 0, 0, tiled=True))  11.8 us
    all_to_all x1, waiting for transfers between devices, shards(): ties = near(lax.all_to_all(ties, NEAR, 0, 0, tiled=True))  5.51 us
    ppermute x1, starting transfers between devices, shards(): one = near(lax.ppermute(current, AXES, swap_route(FIRST)))  1.92 us
    pallas_call x1, Pallas kernels, shards(): call(fetch_kernel, 'fetch', [HBM] * 6, (pltpu.VMEM((Z, 1, V), f32), pltpu...  1.89 us
  transfers between devices with their start and end apart: 3, of which 2 were waited for; matrix products, arithmetic and copies ran while one was open for 0% of the time, Pallas kernels for 3%

profile of v6, /device:TPU:6, one launch (start us, length us, event | category | flops | bytes accessed | tf_op | source)
XLA Modules:
  0.0 73.2 jit_solution(5325067295731643335)
XLA Ops:
  0.6 1.4 %tie_blocks.1 = f32[128,128]{1,0:T(8,128)} custom-call(f32[8,1,1600]{2,1,0:T(1,128)} %x_hbm.3), custom_call_target="tpu_custom_call" | custom-call | tf_op jit(solution)/shard_map/tie_blocks/pallas_call | solution.py:285
  2.0 11.8 %all-to-all-start = ((f32[16,8,128]{2,1,0:T(8,128)}), f32[16,8,128]{2,1,0:T(8,128)S(1)}, u32[]{:S(2)}, u32[]{:S(2)}) async-start(f32[16,8,128]{2,1,0:T(8,128)} %bitcast.16), calls=%async_computation | async-start | bytes 131072 | tf_op jit(solution)/shard_map/all_to_all | solution.py:293
  13.8 1.9 %fetch.1 = (f32[8,1,1600]{2,1,0:T(1,128)S(1)}, f32[8,1,512]{2,1,0:T(1,128)S(1)}, f32[8,1,1600]{2,1,0:T(1,128)S(1)}, s32[80,128]{1,0:T(8,128)S(1)}, bf16[800,1600]{1,0:T(8,128)(2,1)S(1)}) custom-call(f32[8,1,1600]{2,1,0:T(1,128)} %x_hbm.3, f32[8,1,512]{2,1,0:T(1,128)} %dual_hbm.1, f32[8,1,1600]{2,1,0:T(1,128)} %cost_hbm.1, s32[8]{0:T(128)} %sizes_hbm.1, ...), custom_call_target="tpu_custom_call" | custom-call | tf_op jit(solution)/shard_map/fetch/pallas_call | solution.py:294
  15.7 5.5 %all-to-all-done = f32[16,8,128]{2,1,0:T(8,128)S(1)} async-done(((f32[16,8,128]{2,1,0:T(8,128)}), f32[16,8,128]{2,1,0:T(8,128)S(1)}, u32[]{:S(2)}, u32[]{:S(2)}) %all-to-all-start) | async-done | bytes 65568 | tf_op jit(solution)/shard_map/all_to_all | solution.py:293
  21.2 0.2 first_side.1
  21.4 22.9 %all_to_all.33 = bf16[16,8,1920]{2,1,0:T(8,128)(2,1)S(1)} all-to-all(bf16[16,8,1920]{2,1,0:T(8,128)(2,1)S(1)} %bitcast.13), channel_id=1, replica_groups=mesh['xh'=2,'xl'=2,'zh'=4,'core'=2,'y'=8,'zl'=2] {'zl','y'}, dimensions={0} | all-to-all | bytes 983040 | tf_op jit(solution)/shard_map/all_to_all | solution.py:313
  44.3 0.9 %first_product.1 = (f32[104,128]{1,0:T(8,128)S(1)}, f32[56,128]{1,0:T(8,128)S(1)}) custom-call(s32[80,128]{1,0:T(8,128)S(1)} %get-tuple-element.11.meta_ref, bf16[128,1920]{1,0:T(8,128)(2,1)S(1)} %bitcast.9, bf16[800,1600]{1,0:T(8,128)(2,1)S(1)} %get-tuple-element.16.hinv_ref), custom_call_target="tpu_custom_call" | custom-call | tf_op jit(solution)/shard_map/first_product/pallas_call | solution.py:314
  45.2 1.9 %collective-permute-start.1 = (f32[104,128]{1,0:T(8,128)S(1)}, f32[104,128]{1,0:T(8,128)S(1)}, u32[]{:S(2)}, u32[]{:S(2)}) collective-permute-start(f32[104,128]{1,0:T(8,128)S(1)} %get-tuple-element.17.current_ref), channel_id=1, source_target_pairs={{0,16},{1,33},{2,66},{3,67},{4,132},{5,133},{16,0},{17,49},{18,82}... | collective-permute-start | bytes 159752 | tf_op jit(solution)/shard_map/ppermute | solution.py:321
  47.1 0.7 collective-permute-start
  47.8 0.0 collective-permute-done.two_ref
  47.8 0.5 collective-permute-done.1.one_ref
  48.3 1.0 %second_product.1 = bf16[128,1792]{1,0:T(8,128)(2,1)S(1)} custom-call(s32[80,128]{1,0:T(8,128)S(1)} %get-tuple-element.11.meta_ref, bf16[128,1920]{1,0:T(8,128)(2,1)S(1)} %bitcast.10, f32[104,128]{1,0:T(8,128)S(1)} %get-tuple-element.17.current_ref, f32[56,128]{1,0:T(8,128)S(1)} %collective-permute-done.two_ref, ...), custom_call_target="tpu_custom_call" | custom-call | tf_op jit(solution)/shard_map/second_product/pallas_call | solution.py:322
  49.4 23.2 %all_to_all.34 = bf16[16,8,1792]{2,1,0:T(8,128)(2,1)S(1)} all-to-all(bf16[16,8,1792]{2,1,0:T(8,128)(2,1)S(1)} %bitcast.12), channel_id=1, replica_groups=mesh['xh'=2,'xl'=2,'zh'=4,'core'=2,'y'=8,'zl'=2] {'zl','y'}, dimensions={0} | all-to-all | bytes 917504 | tf_op jit(solution)/shard_map/all_to_all | solution.py:325
  72.5 0.7 last_sum.1
Async XLA Ops:
  2.0 19.2 %all-to-all-start = ((f32[16,8,128]{2,1,0:T(8,128)}), f32[16,8,128]{2,1,0:T(8,128)S(1)}, u32[]{:S(2)}, u32[]{:S(2)}) async-start(f32[16,8,128]{2,1,0:T(8,128)} %bitcast.16), calls=%async_computation | async-start | bytes 131072 | tf_op jit(solution)/shard_map/all_to_all | solution.py:293
  45.2 3.1 %collective-permute-start.1 = (f32[104,128]{1,0:T(8,128)S(1)}, f32[104,128]{1,0:T(8,128)S(1)}, u32[]{:S(2)}, u32[]{:S(2)}) collective-permute-start(f32[104,128]{1,0:T(8,128)S(1)} %get-tuple-element.17.current_ref), channel_id=1, source_target_pairs={{0,16},{1,33},{2,66},{3,67},{4,132},{5,133},{16,0},{17,49},{18,82}... | collective-permute-start | bytes 159752 | tf_op jit(solution)/shard_map/ppermute | solution.py:321
  47.1 0.7 collective-permute-start

commit v7 on v6

--- a/solution.py
+++ b/solution.py
@@ -28,7 +28,8 @@
 AXES = ("xh", "xl", "zh", "core", "y", "zl")
 SIZES = (2, 2, 4, 2, 8, 2)
 ZONE = ("xh", "xl", "zh", "core")
-NEAR = ("xl", "zh", "core")
+NEAR = ("zh", "core")
+MEMBERS = 8
 PERIOD = ("y", "zl")
 SLOTS = ("zl", "y")
 ORDER = tuple(range(0, T, 2)) + tuple(range(1, T, 2))
@@ -39,7 +40,7 @@
 
 
 def near_index():
-    return (lax.axis_index("xl") * 4 + lax.axis_index("zh")) * 2 + lax.axis_index("core")
+    return lax.axis_index("zh") * 2 + lax.axis_index("core")
 
 
 def period_index():
@@ -69,7 +70,7 @@
     return values.astype(jnp.bfloat16)
 
 
-def tie_blocks_kernel(x_hbm, ties_hbm, blocks_ref, sems, out_sems):
+def tie_blocks_kernel(x_hbm, ties_hbm, last_hbm, blocks_ref, sems, out_sems):
     me = near_index()
     copies = []
     for r in range(ROUNDS):
@@ -78,9 +79,12 @@
         copies[-1].start()
     sends = []
     for r in range(ROUNDS):
-        slot = pl.multiple_of((me ^ (1 << r)) * Z, Z)
         copies[r].wait()
-        sends.append(pltpu.make_async_copy(blocks_ref.at[r], ties_hbm.at[pl.ds(slot, Z), :], out_sems.at[r]))
+        if r < ROUNDS - 1:
+            there = ties_hbm.at[pl.ds(pl.multiple_of((me ^ (1 << r)) * Z, Z), Z), :]
+        else:
+            there = last_hbm
+        sends.append(pltpu.make_async_copy(blocks_ref.at[r], there, out_sems.at[r]))
         sends[-1].start()
     for send in sends:
         send.wait()
@@ -126,7 +130,7 @@
     return (lane < size).astype(jnp.float32)[:, :V]
 
 
-def first_side_kernel(meta_ref, x_ref, dual_ref, cost_ref, ties_ref, out_ref, dual_out_ref):
+def first_side_kernel(meta_ref, x_ref, dual_ref, cost_ref, ties_ref, last_ref, out_ref, dual_out_ref):
     me = near_index()
     x = x_ref[:, 0, :]
     cost = cost_ref[:, 0, :]
@@ -138,7 +142,8 @@
         mate = meta_ref[MATE_ROW + r * Z : MATE_ROW + (r + 1) * Z, :]
         other = jnp.zeros((Z, W), jnp.float32)
         for z in range(Z):
-            other = jnp.where(mate == z, ties_ref[pl.ds(slot + z, 1), :], other)
+            from_z = ties_ref[pl.ds(slot + z, 1), :] if r < ROUNDS - 1 else last_ref[z : z + 1, :]
+            other = jnp.where(mate == z, from_z, other)
         updated = dual[:, r * W : (r + 1) * W] + 0.5 * (own - other)
         new_duals.append(updated)
         terms.append(0.5 * (own + other) - updated)
@@ -282,15 +287,16 @@
 def shards(x, duals, cost, hinv, sizes, partners):
     f32, bf16 = jnp.float32, jnp.bfloat16
     hinv = jnp.transpose(hinv, (1, 0, 2)).reshape(ROWS * Z, V)
-    ties = call(
+    ties, last = call(
         tie_blocks_kernel,
         "tie_blocks",
         [HBM],
-        pltpu.HBM((T * Z, W), f32),
+        (pltpu.HBM((MEMBERS * Z, W), f32), pltpu.HBM((Z, W), f32)),
         [pltpu.VMEM((ROUNDS, Z, W), f32)] + [pltpu.SemaphoreType.DMA((ROUNDS,))] * 2,
         HBM,
     )(far(x))
     ties = near(lax.all_to_all(ties, NEAR, 0, 0, tiled=True))
+    last = near(lax.ppermute(last, "xl", [(0, 1), (1, 0)]))
     x, duals, cost, meta, hinv = call(
         fetch_kernel,
         "fetch",
@@ -307,9 +313,9 @@
     block, dual = call(
         first_side_kernel,
         "first_side",
-        [VMEM] * 5,
+        [VMEM] * 6,
         (pltpu.VMEM((T * Z, BW), bf16), pltpu.VMEM((Z, TIE), f32)),
-    )(meta, x, duals, cost, ties)
+    )(meta, x, duals, cost, ties, last)
     block = near(lax.all_to_all(block, SLOTS, 0, 0, tiled=True))
     current, part = call(
         first_product_kernel,

time: 74.1 us -> 73.3 us (0.989)
  waiting for transfers between devices: 6.03 us -> 3.92 us
  starting transfers between devices: 14.4 us -> 15.6 us
    all_to_all x1, waiting for transfers between devices: 5.51 us -> 2.33 us  [shards(): ties = near(lax.all_to_all(ties, NEAR, 0, 0, tiled=True))]
    ppermute x0 -> x1, starting transfers between devices: none -> 2.72 us  [shards(): last = near(lax.ppermute(last, 'xl', [(0, 1), (1, 0)]))]
    all_to_all x1, starting transfers between devices: 11.8 us -> 10.3 us  [shards(): ties = near(lax.all_to_all(ties, NEAR, 0, 0, tiled=True))]
    ppermute x0 -> x1, waiting for transfers between devices: none -> 1.07 us  [shards(): last = near(lax.ppermute(last, 'xl', [(0, 1), (1, 0)]))]
  transfers between devices with their start and end apart: 3 -> 4, of which waited for: 2 -> 3; matrix products, arithmetic and copies ran while one was open for 0% -> 0% of each run, Pallas kernels for 3% -> 3%
where the time goes in v7:
time: 73.3 us; the launch traced here: 72.7 us
  blocking collectives  46.4 us (63%)
  starting transfers between devices  15.6 us (21%)
  Pallas kernels  6.06 us (8%)
  waiting for transfers between devices  3.92 us (5%)
    all_to_all x2, blocking collectives, shards(): block = near(lax.all_to_all(block, SLOTS, 0, 0, tiled=True))  46.4 us
    all_to_all x1, starting transfers between devices, shards(): ties = near(lax.all_to_all(ties, NEAR, 0, 0, tiled=True))  10.3 us
    ppermute x1, starting transfers between devices, shards(): last = near(lax.ppermute(last, 'xl', [(0, 1), (1, 0)]))  2.72 us
    all_to_all x1, waiting for transfers between devices, shards(): ties = near(lax.all_to_all(ties, NEAR, 0, 0, tiled=True))  2.33 us
    ppermute x1, starting transfers between devices, shards(): one = near(lax.ppermute(current, AXES, swap_route(FIRST)))  1.92 us
    pallas_call x1, Pallas kernels, shards(): call(fetch_kernel, 'fetch', [HBM] * 6, (pltpu.VMEM((Z, 1, V), f32), pltpu...  1.89 us
  transfers between devices with their start and end apart: 4, of which 3 were waited for; matrix products, arithmetic and copies ran while one was open for 0% of the time, Pallas kernels for 3%

profile of v7, /device:TPU:6, one launch (start us, length us, event | category | flops | bytes accessed | tf_op | source)
XLA Modules:
  0.0 72.7 jit_solution(16006700061256255178)
XLA Ops:
  0.6 1.4 %tie_blocks.1 = (f32[64,128]{1,0:T(8,128)}, f32[8,128]{1,0:T(8,128)}) custom-call(f32[8,1,1600]{2,1,0:T(1,128)} %x_hbm.3), custom_call_target="tpu_custom_call" | custom-call | tf_op jit(solution)/shard_map/tie_blocks/pallas_call | solution.py:290
  2.0 10.3 %all-to-all-start = ((f32[8,8,128]{2,1,0:T(8,128)}), f32[8,8,128]{2,1,0:T(8,128)S(1)}, u32[]{:S(2)}, u32[]{:S(2)}) async-start(f32[8,8,128]{2,1,0:T(8,128)} %bitcast.16), calls=%async_computation | async-start | bytes 65536 | tf_op jit(solution)/shard_map/all_to_all | solution.py:298
  12.4 2.7 %collective-permute-start = (f32[8,128]{1,0:T(8,128)}, f32[8,128]{1,0:T(8,128)S(1)}, u32[]{:S(2)}, u32[]{:S(2)}) collective-permute-start(f32[8,128]{1,0:T(8,128)} %get-tuple-element.18), channel_id=1, source_target_pairs={{0,128},{128,0},{1,129},{129,1},{2,130},{130,2},{3,131},{131,3},{4... | collective-permute-start | bytes 12296 | tf_op jit(solution)/shard_map/ppermute | solution.py:299
  15.1 1.9 %fetch.1 = (f32[8,1,1600]{2,1,0:T(1,128)S(1)}, f32[8,1,512]{2,1,0:T(1,128)S(1)}, f32[8,1,1600]{2,1,0:T(1,128)S(1)}, s32[80,128]{1,0:T(8,128)S(1)}, bf16[800,1600]{1,0:T(8,128)(2,1)S(1)}) custom-call(f32[8,1,1600]{2,1,0:T(1,128)} %x_hbm.3, f32[8,1,512]{2,1,0:T(1,128)} %dual_hbm.1, f32[8,1,1600]{2,1,0:T(1,128)} %cost_hbm.1, s32[8]{0:T(128)} %sizes_hbm.1, ...), custom_call_target="tpu_custom_call" | custom-call | tf_op jit(solution)/shard_map/fetch/pallas_call | solution.py:300
  17.0 1.1 %collective-permute-done.last_ref = f32[8,128]{1,0:T(8,128)S(1)} collective-permute-done((f32[8,128]{1,0:T(8,128)}, f32[8,128]{1,0:T(8,128)S(1)}, u32[]{:S(2)}, u32[]{:S(2)}) %collective-permute-start) | collective-permute-done | bytes 4128 | tf_op jit(solution)/shard_map/ppermute | solution.py:299
  18.1 2.3 %all-to-all-done = f32[8,8,128]{2,1,0:T(8,128)S(1)} async-done(((f32[8,8,128]{2,1,0:T(8,128)}), f32[8,8,128]{2,1,0:T(8,128)S(1)}, u32[]{:S(2)}, u32[]{:S(2)}) %all-to-all-start) | async-done | bytes 32800 | tf_op jit(solution)/shard_map/all_to_all | solution.py:298
  20.4 0.1 first_side.1
  20.5 22.6 %all_to_all.33 = bf16[16,8,1920]{2,1,0:T(8,128)(2,1)S(1)} all-to-all(bf16[16,8,1920]{2,1,0:T(8,128)(2,1)S(1)} %bitcast.13), channel_id=1, replica_groups=mesh['xh'=2,'xl'=2,'zh'=4,'core'=2,'y'=8,'zl'=2] {'zl','y'}, dimensions={0} | all-to-all | bytes 983040 | tf_op jit(solution)/shard_map/all_to_all | solution.py:319
  43.2 0.9 %first_product.1 = (f32[104,128]{1,0:T(8,128)S(1)}, f32[56,128]{1,0:T(8,128)S(1)}) custom-call(s32[80,128]{1,0:T(8,128)S(1)} %get-tuple-element.13.meta_ref, bf16[128,1920]{1,0:T(8,128)(2,1)S(1)} %bitcast.9, bf16[800,1600]{1,0:T(8,128)(2,1)S(1)} %get-tuple-element.20.hinv_ref), custom_call_target="tpu_custom_call" | custom-call | tf_op jit(solution)/shard_map/first_product/pallas_call | solution.py:320
  44.1 1.9 %collective-permute-start.2 = (f32[104,128]{1,0:T(8,128)S(1)}, f32[104,128]{1,0:T(8,128)S(1)}, u32[]{:S(2)}, u32[]{:S(2)}) collective-permute-start(f32[104,128]{1,0:T(8,128)S(1)} %get-tuple-element.21.current_ref), channel_id=1, source_target_pairs={{0,16},{1,33},{2,66},{3,67},{4,132},{5,133},{16,0},{17,49},{18,82}... | collective-permute-start | bytes 159752 | tf_op jit(solution)/shard_map/ppermute | solution.py:327
  46.0 0.7 collective-permute-start.1
  46.7 0.0 collective-permute-done.1.two_ref
  46.7 0.5 collective-permute-done.2.one_ref
  47.2 1.0 %second_product.1 = bf16[128,1792]{1,0:T(8,128)(2,1)S(1)} custom-call(s32[80,128]{1,0:T(8,128)S(1)} %get-tuple-element.13.meta_ref, bf16[128,1920]{1,0:T(8,128)(2,1)S(1)} %bitcast.10, f32[104,128]{1,0:T(8,128)S(1)} %get-tuple-element.21.current_ref, f32[56,128]{1,0:T(8,128)S(1)} %collective-permute-done.1.two_ref, ...), custom_call_target="tpu_custom_call" | custom-call | tf_op jit(solution)/shard_map/second_product/pallas_call | solution.py:328
  48.2 23.7 %all_to_all.34 = bf16[16,8,1792]{2,1,0:T(8,128)(2,1)S(1)} all-to-all(bf16[16,8,1792]{2,1,0:T(8,128)(2,1)S(1)} %bitcast.12), channel_id=1, replica_groups=mesh['xh'=2,'xl'=2,'zh'=4,'core'=2,'y'=8,'zl'=2] {'zl','y'}, dimensions={0} | all-to-all | bytes 917504 | tf_op jit(solution)/shard_map/all_to_all | solution.py:331
  72.0 0.7 last_sum.1
Async XLA Ops:
  2.0 18.3 %all-to-all-start = ((f32[8,8,128]{2,1,0:T(8,128)}), f32[8,8,128]{2,1,0:T(8,128)S(1)}, u32[]{:S(2)}, u32[]{:S(2)}) async-start(f32[8,8,128]{2,1,0:T(8,128)} %bitcast.16), calls=%async_computation | async-start | bytes 65536 | tf_op jit(solution)/shard_map/all_to_all | solution.py:298
  12.4 5.7 %collective-permute-start = (f32[8,128]{1,0:T(8,128)}, f32[8,128]{1,0:T(8,128)S(1)}, u32[]{:S(2)}, u32[]{:S(2)}) collective-permute-start(f32[8,128]{1,0:T(8,128)} %get-tuple-element.18), channel_id=1, source_target_pairs={{0,128},{128,0},{1,129},{129,1},{2,130},{130,2},{3,131},{131,3},{4... | collective-permute-start | bytes 12296 | tf_op jit(solution)/shard_map/ppermute | solution.py:299
  44.1 3.1 %collective-permute-start.2 = (f32[104,128]{1,0:T(8,128)S(1)}, f32[104,128]{1,0:T(8,128)S(1)}, u32[]{:S(2)}, u32[]{:S(2)}) collective-permute-start(f32[104,128]{1,0:T(8,128)S(1)} %get-tuple-element.21.current_ref), channel_id=1, source_target_pairs={{0,16},{1,33},{2,66},{3,67},{4,132},{5,133},{16,0},{17,49},{18,82}... | collective-permute-start | bytes 159752 | tf_op jit(solution)/shard_map/ppermute | solution.py:327
  46.0 0.7 collective-permute-start.1

commit v8 on v7

--- a/solution.py
+++ b/solution.py
@@ -195,24 +195,37 @@
     second_ref[...] = jnp.where(period_index() == 3, current[RP - SECOND_ROWS :], current[:SECOND_ROWS])
 
 
-def second_product_kernel(meta_ref, block_ref, current_ref, two_ref, one_ref, hinv_ref, out_ref):
-    k = period_index()
+def rounds_here(k):
     first_round = jnp.where(k == 0, 0, jnp.where(k == 1, 1, jnp.where(k <= 3, 2, 3)))
     second_round = jnp.where(k == 1, 0, jnp.where(k == 2, 1, jnp.where(k == 3, 3, 0)))
+    return first_round, second_round
+
+
+def second_side_kernel(meta_ref, block_ref, current_ref, side_ref, picks_ref):
+    k = period_index()
     current = current_ref[...]
     later = block_ref[:, TAIL:RAMP_AT].astype(jnp.float32).T[V - TAIL :]
     blank = jnp.zeros((RP - LOW, T * Z), jnp.float32)
     later = jnp.concatenate([later[:ROWS], blank[: RP - ROWS]], axis=0) + jnp.concatenate([later[ROWS:], blank], axis=0)
     place = lax.broadcasted_iota(jnp.int32, (T * Z, T * Z), 0)
     group = lax.broadcasted_iota(jnp.int32, (T * Z, T * Z), 1) & ~(Z - 1)
-
-    def pick(round_index):
+    for i, round_index in enumerate(rounds_here(k)):
         mate = meta_ref[pl.ds(MATE_LANE + round_index * Z, 1), :]
-        return (place == group + mate).astype(jnp.float32)
-
-    row = lax.broadcasted_iota(jnp.int32, (RP, T * Z), 0)
+        picks_ref[i * T * Z : (i + 1) * T * Z, :] = (place == group + mate).astype(jnp.float32)
     lane = lax.broadcasted_iota(jnp.int32, (RP, T * Z), 1)
-    entry = row + k * ROWS
+    entry = lax.broadcasted_iota(jnp.int32, (RP, T * Z), 0) + k * ROWS
+    beside = pltpu.roll(current, HALF, 1)
+    before = jnp.where(lane < Z, 0.0, pltpu.roll(beside, Z, 1))
+    after = jnp.where(lane >= (T - 1) * Z, 0.0, pltpu.roll(beside, (T - 1) * Z, 1))
+    ramp = jnp.where((entry >= TIE) & (entry < RAMP), 0.5 * (beside + jnp.where(lane < HALF, before, after)), 0.0)
+    side_ref[...] = 0.5 * current - later + ramp
+
+
+def second_product_kernel(meta_ref, side_ref, picks_ref, current_ref, two_ref, one_ref, hinv_ref, out_ref):
+    k = period_index()
+    first_round, second_round = rounds_here(k)
+    current = current_ref[...]
+    entry = lax.broadcasted_iota(jnp.int32, (RP, T * Z), 0) + k * ROWS
     round_of = entry >> 7
     tie = entry < TIE
     blank = jnp.zeros((RP - SECOND_ROWS, T * Z), jnp.float32)
@@ -228,15 +241,9 @@
         ],
         axis=1,
     )
-    picks = jnp.concatenate([pick(first_round), pick(second_round)], axis=0)
-    other = jnp.dot(received, picks, preferred_element_type=jnp.float32, precision=lax.Precision.HIGHEST)
-    beside = pltpu.roll(current, HALF, 1)
-    before = jnp.where(lane < Z, 0.0, pltpu.roll(beside, Z, 1))
-    after = jnp.where(lane >= (T - 1) * Z, 0.0, pltpu.roll(beside, (T - 1) * Z, 1))
-    ramp = jnp.where((entry >= TIE) & (entry < RAMP), 0.5 * (beside + jnp.where(lane < HALF, before, after)), 0.0)
-    right = 0.5 * current - later + jnp.where(tie, other, ramp)
+    other = jnp.dot(received, picks_ref[...], preferred_element_type=jnp.float32, precision=lax.Precision.HIGHEST)
     size = meta_ref[SIZE_LANE : SIZE_LANE + 1, :]
-    right = jnp.where(entry < size, right, 0.0)[:ROWS]
+    right = jnp.where(entry < size, side_ref[...] + other, 0.0)[:ROWS]
     side = rounded(jnp.where(zone_match()[None], right[:, None, :], 0.0).reshape(ROWS * Z, T * Z))
     step = jnp.where(tie, 0.5 * (current - other), 0.0)
     step = jnp.concatenate([step, jnp.zeros((W - RP, T * Z), jnp.float32)], axis=0).T
@@ -325,8 +332,14 @@
     )(meta, block, hinv)
     two = near(lax.ppermute(part, AXES, swap_route(SECOND)))
     one = near(lax.ppermute(current, AXES, swap_route(FIRST)))
-    block = call(second_product_kernel, "second_product", [VMEM] * 6, pltpu.VMEM((T * Z, DW), bf16))(
-        meta, block, current, two, one, hinv
+    side, picks = call(
+        second_side_kernel,
+        "second_side",
+        [VMEM] * 3,
+        (pltpu.VMEM((RP, T * Z), f32), pltpu.VMEM((2 * T * Z, T * Z), f32)),
+    )(meta, block, current)
+    block = call(second_product_kernel, "second_product", [VMEM] * 7, pltpu.VMEM((T * Z, DW), bf16))(
+        meta, side, picks, current, two, one, hinv
     )
     block = near(lax.all_to_all(block, SLOTS, 0, 0, tiled=True))
     shape = jax.ShapeDtypeStruct

time: 73.3 us -> 73.1 us (level)
  no operation moved by 1% of the time
where the time goes in v8:
time: 73.1 us; the launch traced here: 72.6 us
  blocking collectives  46.4 us (63%)
  starting transfers between devices  15.6 us (21%)
  Pallas kernels  6.12 us (8%)
  waiting for transfers between devices  3.73 us (5%)
    all_to_all x2, blocking collectives, shards(): block = near(lax.all_to_all(block, SLOTS, 0, 0, tiled=True))  46.4 us
    all_to_all x1, starting transfers between devices, shards(): ties = near(lax.all_to_all(ties, NEAR, 0, 0, tiled=True))  10.3 us
    ppermute x1, starting transfers between devices, shards(): last = near(lax.ppermute(last, 'xl', [(0, 1), (1, 0)]))  2.72 us
    all_to_all x1, waiting for transfers between devices, shards(): ties = near(lax.all_to_all(ties, NEAR, 0, 0, tiled=True))  2.33 us
    ppermute x1, starting transfers between devices, shards(): one = near(lax.ppermute(current, AXES, swap_route(FIRST)))  1.92 us
    pallas_call x1, Pallas kernels, shards(): call(fetch_kernel, 'fetch', [HBM] * 6, (pltpu.VMEM((Z, 1, V), f32), pltpu...  1.89 us
  transfers between devices with their start and end apart: 4, of which 3 were waited for; matrix products, arithmetic and copies ran while one was open for 0% of the time, Pallas kernels for 3%

profile of v8, /device:TPU:6, one launch (start us, length us, event | category | flops | bytes accessed | tf_op | source)
XLA Modules:
  0.0 72.6 jit_solution(12571893267970746588)
XLA Ops:
  0.6 1.4 %tie_blocks.1 = (f32[64,128]{1,0:T(8,128)}, f32[8,128]{1,0:T(8,128)}) custom-call(f32[8,1,1600]{2,1,0:T(1,128)} %x_hbm.3), custom_call_target="tpu_custom_call" | custom-call | tf_op jit(solution)/shard_map/tie_blocks/pallas_call | solution.py:297
  2.0 10.3 %all-to-all-start = ((f32[8,8,128]{2,1,0:T(8,128)}), f32[8,8,128]{2,1,0:T(8,128)S(1)}, u32[]{:S(2)}, u32[]{:S(2)}) async-start(f32[8,8,128]{2,1,0:T(8,128)} %bitcast.16), calls=%async_computation | async-start | bytes 65536 | tf_op jit(solution)/shard_map/all_to_all | solution.py:305
  12.4 2.7 %collective-permute-start = (f32[8,128]{1,0:T(8,128)}, f32[8,128]{1,0:T(8,128)S(1)}, u32[]{:S(2)}, u32[]{:S(2)}) collective-permute-start(f32[8,128]{1,0:T(8,128)} %get-tuple-element.20), channel_id=1, source_target_pairs={{0,128},{128,0},{1,129},{129,1},{2,130},{130,2},{3,131},{131,3},{4... | collective-permute-start | bytes 12296 | tf_op jit(solution)/shard_map/ppermute | solution.py:306
  15.1 1.9 %fetch.1 = (f32[8,1,1600]{2,1,0:T(1,128)S(1)}, f32[8,1,512]{2,1,0:T(1,128)S(1)}, f32[8,1,1600]{2,1,0:T(1,128)S(1)}, s32[80,128]{1,0:T(8,128)S(1)}, bf16[800,1600]{1,0:T(8,128)(2,1)S(1)}) custom-call(f32[8,1,1600]{2,1,0:T(1,128)} %x_hbm.3, f32[8,1,512]{2,1,0:T(1,128)} %dual_hbm.1, f32[8,1,1600]{2,1,0:T(1,128)} %cost_hbm.1, s32[8]{0:T(128)} %sizes_hbm.1, ...), custom_call_target="tpu_custom_call" | custom-call | tf_op jit(solution)/shard_map/fetch/pallas_call | solution.py:307
  17.0 1.1 %collective-permute-done.last_ref = f32[8,128]{1,0:T(8,128)S(1)} collective-permute-done((f32[8,128]{1,0:T(8,128)}, f32[8,128]{1,0:T(8,128)S(1)}, u32[]{:S(2)}, u32[]{:S(2)}) %collective-permute-start) | collective-permute-done | bytes 4128 | tf_op jit(solution)/shard_map/ppermute | solution.py:306
  18.1 2.3 %all-to-all-done = f32[8,8,128]{2,1,0:T(8,128)S(1)} async-done(((f32[8,8,128]{2,1,0:T(8,128)}), f32[8,8,128]{2,1,0:T(8,128)S(1)}, u32[]{:S(2)}, u32[]{:S(2)}) %all-to-all-start) | async-done | bytes 32800 | tf_op jit(solution)/shard_map/all_to_all | solution.py:305
  20.4 0.1 first_side.1
  20.5 22.6 %all_to_all.33 = bf16[16,8,1920]{2,1,0:T(8,128)(2,1)S(1)} all-to-all(bf16[16,8,1920]{2,1,0:T(8,128)(2,1)S(1)} %bitcast.13), channel_id=1, replica_groups=mesh['xh'=2,'xl'=2,'zh'=4,'core'=2,'y'=8,'zl'=2] {'zl','y'}, dimensions={0} | all-to-all | bytes 983040 | tf_op jit(solution)/shard_map/all_to_all | solution.py:326
  43.2 0.9 %first_product.1 = (f32[104,128]{1,0:T(8,128)S(1)}, f32[56,128]{1,0:T(8,128)S(1)}) custom-call(s32[80,128]{1,0:T(8,128)S(1)} %get-tuple-element.15.meta_ref, bf16[128,1920]{1,0:T(8,128)(2,1)S(1)} %bitcast.9, bf16[800,1600]{1,0:T(8,128)(2,1)S(1)} %get-tuple-element.22.hinv_ref), custom_call_target="tpu_custom_call" | custom-call | tf_op jit(solution)/shard_map/first_product/pallas_call | solution.py:327
  44.1 1.9 %collective-permute-start.2 = (f32[104,128]{1,0:T(8,128)S(1)}, f32[104,128]{1,0:T(8,128)S(1)}, u32[]{:S(2)}, u32[]{:S(2)}) collective-permute-start(f32[104,128]{1,0:T(8,128)S(1)} %get-tuple-element.23.current_ref), channel_id=1, source_target_pairs={{0,16},{1,33},{2,66},{3,67},{4,132},{5,133},{16,0},{17,49},{18,82}... | collective-permute-start | bytes 159752 | tf_op jit(solution)/shard_map/ppermute | solution.py:334
  46.0 0.7 collective-permute-start.1
  46.7 0.2 second_side.1
  46.9 0.0 collective-permute-done.1.two_ref
  46.9 0.3 collective-permute-done.2.one_ref
  47.2 0.9 %second_product.1 = bf16[128,1792]{1,0:T(8,128)(2,1)S(1)} custom-call(s32[80,128]{1,0:T(8,128)S(1)} %get-tuple-element.15.meta_ref, f32[104,128]{1,0:T(8,128)S(1)} %get-tuple-element.24.side_ref, f32[256,128]{1,0:T(8,128)S(1)} %get-tuple-element.25.picks_ref, f32[104,128]{1,0:T(8,128)S(1)} %get-tuple-element.23.current_ref, ...), custom_call_target="tpu_custom_call" | custom-call | tf_op jit(solution)/shard_map/second_product/pallas_call | solution.py:341
  48.1 23.7 %all_to_all.34 = bf16[16,8,1792]{2,1,0:T(8,128)(2,1)S(1)} all-to-all(bf16[16,8,1792]{2,1,0:T(8,128)(2,1)S(1)} %bitcast.12), channel_id=1, replica_groups=mesh['xh'=2,'xl'=2,'zh'=4,'core'=2,'y'=8,'zl'=2] {'zl','y'}, dimensions={0} | all-to-all | bytes 917504 | tf_op jit(solution)/shard_map/all_to_all | solution.py:344
  71.9 0.7 last_sum.1
Async XLA Ops:
  2.0 18.3 %all-to-all-start = ((f32[8,8,128]{2,1,0:T(8,128)}), f32[8,8,128]{2,1,0:T(8,128)S(1)}, u32[]{:S(2)}, u32[]{:S(2)}) async-start(f32[8,8,128]{2,1,0:T(8,128)} %bitcast.16), calls=%async_computation | async-start | bytes 65536 | tf_op jit(solution)/shard_map/all_to_all | solution.py:305
  12.4 5.7 %collective-permute-start = (f32[8,128]{1,0:T(8,128)}, f32[8,128]{1,0:T(8,128)S(1)}, u32[]{:S(2)}, u32[]{:S(2)}) collective-permute-start(f32[8,128]{1,0:T(8,128)} %get-tuple-element.20), channel_id=1, source_target_pairs={{0,128},{128,0},{1,129},{129,1},{2,130},{130,2},{3,131},{131,3},{4... | collective-permute-start | bytes 12296 | tf_op jit(solution)/shard_map/ppermute | solution.py:306
  44.1 3.1 %collective-permute-start.2 = (f32[104,128]{1,0:T(8,128)S(1)}, f32[104,128]{1,0:T(8,128)S(1)}, u32[]{:S(2)}, u32[]{:S(2)}) collective-permute-start(f32[104,128]{1,0:T(8,128)S(1)} %get-tuple-element.23.current_ref), channel_id=1, source_target_pairs={{0,16},{1,33},{2,66},{3,67},{4,132},{5,133},{16,0},{17,49},{18,82}... | collective-permute-start | bytes 159752 | tf_op jit(solution)/shard_map/ppermute | solution.py:334
  46.0 0.9 %collective-permute-start.1 = (f32[56,128]{1,0:T(8,128)S(1)}, f32[56,128]{1,0:T(8,128)S(1)}, u32[]{:S(2)}, u32[]{:S(2)}) collective-permute-start(f32[56,128]{1,0:T(8,128)S(1)} %get-tuple-element.26), channel_id=1, source_target_pairs={{1,17},{2,34},{3,131},{17,1},{18,50},{19,147},{33,49},{34,2},{35,1... | collective-permute-start | bytes 86024 | tf_op jit(solution)/shard_map/ppermute | solution.py:333

commit v9 on v7

--- a/solution.py
+++ b/solution.py
@@ -28,8 +28,9 @@
 AXES = ("xh", "xl", "zh", "core", "y", "zl")
 SIZES = (2, 2, 4, 2, 8, 2)
 ZONE = ("xh", "xl", "zh", "core")
-NEAR = ("zh", "core")
+NEAR = ("core", "zh")
 MEMBERS = 8
+FLIP = (4, 1, 2, 0)
 PERIOD = ("y", "zl")
 SLOTS = ("zl", "y")
 ORDER = tuple(range(0, T, 2)) + tuple(range(1, T, 2))
@@ -40,7 +41,7 @@
 
 
 def near_index():
-    return lax.axis_index("zh") * 2 + lax.axis_index("core")
+    return lax.axis_index("core") * 4 + lax.axis_index("zh")
 
 
 def period_index():
@@ -81,7 +82,7 @@
     for r in range(ROUNDS):
         copies[r].wait()
         if r < ROUNDS - 1:
-            there = ties_hbm.at[pl.ds(pl.multiple_of((me ^ (1 << r)) * Z, Z), Z), :]
+            there = ties_hbm.at[pl.ds(pl.multiple_of((me ^ FLIP[r]) * Z, Z), Z), :]
         else:
             there = last_hbm
         sends.append(pltpu.make_async_copy(blocks_ref.at[r], there, out_sems.at[r]))
@@ -138,7 +139,7 @@
     terms, new_duals = [], []
     for r in range(ROUNDS):
         own = x[:, r * W : (r + 1) * W]
-        slot = (me ^ (1 << r)) * Z
+        slot = (me ^ FLIP[r]) * Z
         mate = meta_ref[MATE_ROW + r * Z : MATE_ROW + (r + 1) * Z, :]
         other = jnp.zeros((Z, W), jnp.float32)
         for z in range(Z):

time: 73.3 us -> 73.4 us (level)
  no operation moved by 1% of the time
where the time goes in v9:
time: 73.4 us; the launch traced here: 72.6 us
  blocking collectives  46.5 us (63%)
  starting transfers between devices  15.6 us (21%)
  Pallas kernels  6.06 us (8%)
  waiting for transfers between devices  3.71 us (5%)
    all_to_all x2, blocking collectives, shards(): block = near(lax.all_to_all(block, SLOTS, 0, 0, tiled=True))  46.5 us
    all_to_all x1, starting transfers between devices, shards(): ties = near(lax.all_to_all(ties, NEAR, 0, 0, tiled=True))  10.3 us
    ppermute x1, starting transfers between devices, shards(): last = near(lax.ppermute(last, 'xl', [(0, 1), (1, 0)]))  2.72 us
    all_to_all x1, waiting for transfers between devices, shards(): ties = near(lax.all_to_all(ties, NEAR, 0, 0, tiled=True))  2.12 us
    ppermute x1, starting transfers between devices, shards(): one = near(lax.ppermute(current, AXES, swap_route(FIRST)))  1.92 us
    pallas_call x1, Pallas kernels, shards(): call(fetch_kernel, 'fetch', [HBM] * 6, (pltpu.VMEM((Z, 1, V), f32), pltpu...  1.89 us
  transfers between devices with their start and end apart: 4, of which 3 were waited for; matrix products, arithmetic and copies ran while one was open for 0% of the time, Pallas kernels for 3%

profile of v9, /device:TPU:6, one launch (start us, length us, event | category | flops | bytes accessed | tf_op | source)
XLA Modules:
  0.0 72.6 jit_solution(1255524851145996740)
XLA Ops:
  0.6 1.4 %tie_blocks.1 = (f32[64,128]{1,0:T(8,128)}, f32[8,128]{1,0:T(8,128)}) custom-call(f32[8,1,1600]{2,1,0:T(1,128)} %x_hbm.3), custom_call_target="tpu_custom_call" | custom-call | tf_op jit(solution)/shard_map/tie_blocks/pallas_call | solution.py:291
  2.0 10.3 %all-to-all-start = ((f32[8,8,128]{2,1,0:T(8,128)}), f32[8,8,128]{2,1,0:T(8,128)S(1)}, u32[]{:S(2)}, u32[]{:S(2)}) async-start(f32[8,8,128]{2,1,0:T(8,128)} %bitcast.16), calls=%async_computation | async-start | bytes 65536 | tf_op jit(solution)/shard_map/all_to_all | solution.py:299
  12.4 2.7 %collective-permute-start = (f32[8,128]{1,0:T(8,128)}, f32[8,128]{1,0:T(8,128)S(1)}, u32[]{:S(2)}, u32[]{:S(2)}) collective-permute-start(f32[8,128]{1,0:T(8,128)} %get-tuple-element.18), channel_id=1, source_target_pairs={{0,128},{128,0},{1,129},{129,1},{2,130},{130,2},{3,131},{131,3},{4... | collective-permute-start | bytes 12296 | tf_op jit(solution)/shard_map/ppermute | solution.py:300
  15.1 1.9 %fetch.1 = (f32[8,1,1600]{2,1,0:T(1,128)S(1)}, f32[8,1,512]{2,1,0:T(1,128)S(1)}, f32[8,1,1600]{2,1,0:T(1,128)S(1)}, s32[80,128]{1,0:T(8,128)S(1)}, bf16[800,1600]{1,0:T(8,128)(2,1)S(1)}) custom-call(f32[8,1,1600]{2,1,0:T(1,128)} %x_hbm.3, f32[8,1,512]{2,1,0:T(1,128)} %dual_hbm.1, f32[8,1,1600]{2,1,0:T(1,128)} %cost_hbm.1, s32[8]{0:T(128)} %sizes_hbm.1, ...), custom_call_target="tpu_custom_call" | custom-call | tf_op jit(solution)/shard_map/fetch/pallas_call | solution.py:301
  17.0 1.1 %collective-permute-done.last_ref = f32[8,128]{1,0:T(8,128)S(1)} collective-permute-done((f32[8,128]{1,0:T(8,128)}, f32[8,128]{1,0:T(8,128)S(1)}, u32[]{:S(2)}, u32[]{:S(2)}) %collective-permute-start) | collective-permute-done | bytes 4128 | tf_op jit(solution)/shard_map/ppermute | solution.py:300
  18.1 2.1 %all-to-all-done = f32[8,8,128]{2,1,0:T(8,128)S(1)} async-done(((f32[8,8,128]{2,1,0:T(8,128)}), f32[8,8,128]{2,1,0:T(8,128)S(1)}, u32[]{:S(2)}, u32[]{:S(2)}) %all-to-all-start) | async-done | bytes 32800 | tf_op jit(solution)/shard_map/all_to_all | solution.py:299
  20.2 0.1 first_side.1
  20.3 23.1 %all_to_all.33 = bf16[16,8,1920]{2,1,0:T(8,128)(2,1)S(1)} all-to-all(bf16[16,8,1920]{2,1,0:T(8,128)(2,1)S(1)} %bitcast.13), channel_id=1, replica_groups=mesh['xh'=2,'xl'=2,'zh'=4,'core'=2,'y'=8,'zl'=2] {'zl','y'}, dimensions={0} | all-to-all | bytes 983040 | tf_op jit(solution)/shard_map/all_to_all | solution.py:320
  43.4 0.9 %first_product.1 = (f32[104,128]{1,0:T(8,128)S(1)}, f32[56,128]{1,0:T(8,128)S(1)}) custom-call(s32[80,128]{1,0:T(8,128)S(1)} %get-tuple-element.13.meta_ref, bf16[128,1920]{1,0:T(8,128)(2,1)S(1)} %bitcast.9, bf16[800,1600]{1,0:T(8,128)(2,1)S(1)} %get-tuple-element.20.hinv_ref), custom_call_target="tpu_custom_call" | custom-call | tf_op jit(solution)/shard_map/first_product/pallas_call | solution.py:321
  44.3 1.9 %collective-permute-start.2 = (f32[104,128]{1,0:T(8,128)S(1)}, f32[104,128]{1,0:T(8,128)S(1)}, u32[]{:S(2)}, u32[]{:S(2)}) collective-permute-start(f32[104,128]{1,0:T(8,128)S(1)} %get-tuple-element.21.current_ref), channel_id=1, source_target_pairs={{0,16},{1,33},{2,66},{3,67},{4,132},{5,133},{16,0},{17,49},{18,82}... | collective-permute-start | bytes 159752 | tf_op jit(solution)/shard_map/ppermute | solution.py:328
  46.2 0.7 collective-permute-start.1
  46.9 0.0 collective-permute-done.1.two_ref
  46.9 0.5 collective-permute-done.2.one_ref
  47.4 1.0 %second_product.1 = bf16[128,1792]{1,0:T(8,128)(2,1)S(1)} custom-call(s32[80,128]{1,0:T(8,128)S(1)} %get-tuple-element.13.meta_ref, bf16[128,1920]{1,0:T(8,128)(2,1)S(1)} %bitcast.10, f32[104,128]{1,0:T(8,128)S(1)} %get-tuple-element.21.current_ref, f32[56,128]{1,0:T(8,128)S(1)} %collective-permute-done.1.two_ref, ...), custom_call_target="tpu_custom_call" | custom-call | tf_op jit(solution)/shard_map/second_product/pallas_call | solution.py:329
  48.5 23.4 %all_to_all.34 = bf16[16,8,1792]{2,1,0:T(8,128)(2,1)S(1)} all-to-all(bf16[16,8,1792]{2,1,0:T(8,128)(2,1)S(1)} %bitcast.12), channel_id=1, replica_groups=mesh['xh'=2,'xl'=2,'zh'=4,'core'=2,'y'=8,'zl'=2] {'zl','y'}, dimensions={0} | all-to-all | bytes 917504 | tf_op jit(solution)/shard_map/all_to_all | solution.py:332
  71.9 0.7 last_sum.1
Async XLA Ops:
  2.0 18.1 %all-to-all-start = ((f32[8,8,128]{2,1,0:T(8,128)}), f32[8,8,128]{2,1,0:T(8,128)S(1)}, u32[]{:S(2)}, u32[]{:S(2)}) async-start(f32[8,8,128]{2,1,0:T(8,128)} %bitcast.16), calls=%async_computation | async-start | bytes 65536 | tf_op jit(solution)/shard_map/all_to_all | solution.py:299
  12.4 5.7 %collective-permute-start = (f32[8,128]{1,0:T(8,128)}, f32[8,128]{1,0:T(8,128)S(1)}, u32[]{:S(2)}, u32[]{:S(2)}) collective-permute-start(f32[8,128]{1,0:T(8,128)} %get-tuple-element.18), channel_id=1, source_target_pairs={{0,128},{128,0},{1,129},{129,1},{2,130},{130,2},{3,131},{131,3},{4... | collective-permute-start | bytes 12296 | tf_op jit(solution)/shard_map/ppermute | solution.py:300
  44.3 3.1 %collective-permute-start.2 = (f32[104,128]{1,0:T(8,128)S(1)}, f32[104,128]{1,0:T(8,128)S(1)}, u32[]{:S(2)}, u32[]{:S(2)}) collective-permute-start(f32[104,128]{1,0:T(8,128)S(1)} %get-tuple-element.21.current_ref), channel_id=1, source_target_pairs={{0,16},{1,33},{2,66},{3,67},{4,132},{5,133},{16,0},{17,49},{18,82}... | collective-permute-start | bytes 159752 | tf_op jit(solution)/shard_map/ppermute | solution.py:328
  46.2 0.7 collective-permute-start.1
